TPU v7x, 512 devices: a whole 4x4x16 slice. The times are simulated.
512 devices in a mesh: dp: 32 (over y, x, core), seq: 16 (over z).
Axes of the slice: x: 4, y: 4, z: 16, core: 2. Of those that a mesh axis runs over, the one named last changes fastest.
Arguments:
- queries: bfloat16 [32, 2048, 2048], P('dp', 'seq')
- keys: bfloat16 [32, 2048, 2048], P('dp', 'seq')
- events: bfloat16 [32, 2048, 2048], P('dp', 'seq'), may hold values from -6 to 6
- out_grad: bfloat16 [32, 2048, 2048], P('dp', 'seq'), may hold values from -6 to 6
- segment_ids: int32 [32, 2048], P('dp', 'seq'), may hold values from 0 to 63, never falling along the last dimension, each value on 1 to 512 neighbouring positions
- block_list: int32 [32, 16, 4], P('dp'), may hold values from 0 to 15, as said below
- conv_weight: float32 [64, 2048], replicated, may hold values from -0.75 to 0.75
Outputs:
- query_grad: bfloat16 [32, 2048, 2048], P('dp', 'seq')
- key_grad: bfloat16 [32, 2048, 2048], P('dp', 'seq')
- event_grad: bfloat16 [32, 2048, 2048], P('dp', 'seq')
- filter_grad: float32 [64, 2048], replicated
Inputs may be any that keep to these rules, and one draw needn't show every extreme that they name: `block_list`: entry 0 for query block b is b itself; every entry for block b lies in 0 .. b; entries may repeat.
All inputs are finite; a program needn't handle non-finite values.
Results may differ from a plain program's by a relative error of at most 0.015.
Values may be sent and summed in bfloat16 or wider, within the bound.
A program may use at most 64 MiB of HBM per device.

v0:
```python
import jax
import jax.numpy as jnp
from jax import lax
from jax.sharding import PartitionSpec as P

HD = 64
BLOCK = 128


def shifted(value, axis, steps):
    count = lax.axis_size(axis)
    initial, last = (max(0, -steps), min(count, count - steps))
    return lax.ppermute(value, axis, [(source, source + steps) for source in range(initial, last)])


def contract(form, left, right, exact):
    if exact:
        return jnp.einsum(
            form, left, right, precision=lax.Precision.HIGHEST, preferred_element_type=jnp.float32
        )
    return jnp.einsum(form, left, right, preferred_element_type=jnp.float32)


def causal_conv(padded, ids_ext, weight, count):
    taps = weight.shape[0]
    own = ids_ext[taps - 1 : taps - 1 + count]
    total = jnp.zeros((count, padded.shape[1]), jnp.float32)
    for step in range(taps):
        begin = taps - 1 - step
        piece = padded[begin : begin + count].astype(jnp.float32)
        match = (ids_ext[begin : begin + count] == own)[:, None]
        total = total + jnp.where(match, piece * weight[step : step + 1], 0.0)
    return total


def anti_conv(padded, ids_ext, weight, count):
    taps = weight.shape[0]
    own = ids_ext[0:count]
    total = jnp.zeros((count, padded.shape[1]), jnp.float32)
    for step in range(taps):
        piece = padded[step : step + count].astype(jnp.float32)
        match = (ids_ext[step : step + count] == own)[:, None]
        total = total + jnp.where(match, piece * weight[step : step + 1], 0.0)
    return total


def tap_gradient(grad, padded, ids_ext, taps):
    count = grad.shape[0]
    own = ids_ext[taps - 1 : taps - 1 + count]
    grad_wide = grad.astype(jnp.float32)
    sums = []
    for step in range(taps):
        begin = taps - 1 - step
        piece = padded[begin : begin + count].astype(jnp.float32)
        match = (ids_ext[begin : begin + count] == own)[:, None]
        sums.append(jnp.sum(jnp.where(match, piece * grad_wide, 0.0), axis=0))
    return jnp.stack(sums, axis=0)


def block_attention(query, key_rows, value, grad, ids, blist, block):
    tokens, head_dim = query.shape
    nblk = tokens // block
    nsel = blist.shape[1]
    scale = head_dim ** (-0.5)
    same = blist[:, :, None] == blist[:, None, :]
    before = jnp.arange(nsel)[None, :, None] > jnp.arange(nsel)[None, None, :]
    fresh = jnp.logical_not(jnp.any(same & before, axis=2))
    chosen = (blist[:, :, None] == jnp.arange(nblk, dtype=jnp.int32)[None, None, :]) & fresh[
        :, :, None
    ]
    picker = chosen.astype(jnp.bfloat16)
    q_blk = query.reshape(nblk, block, head_dim)
    k_blk = key_rows.reshape(nblk, block, head_dim)
    v_blk = value.reshape(nblk, block, head_dim)
    g_blk = grad.reshape(nblk, block, head_dim)
    k_sel = contract("bjc,cmd->bjmd", picker, k_blk, False).astype(jnp.bfloat16)
    v_sel = contract("bjc,cmd->bjmd", picker, v_blk, False).astype(jnp.bfloat16)
    id_blk = ids.reshape(nblk, block)
    id_sel = jnp.sum(jnp.where(chosen[:, :, :, None], id_blk[None, None, :, :], 0), axis=2)
    q_pos = (
        jnp.arange(nblk, dtype=jnp.int32)[:, None] * block
        + jnp.arange(block, dtype=jnp.int32)[None, :]
    )
    k_pos = blist[:, :, None] * block + jnp.arange(block, dtype=jnp.int32)[None, None, :]
    allowed = (
        fresh[:, None, :, None]
        & (k_pos[:, None] <= q_pos[:, :, None, None])
        & (id_sel[:, None] == id_blk[:, :, None, None])
    )
    scores = contract("bid,bjmd->bijm", q_blk, k_sel, False) * scale
    scores = jnp.where(allowed, scores, -1e30)
    top = jnp.max(scores, axis=(2, 3), keepdims=True)
    weights = jnp.where(allowed, jnp.exp(scores - top), 0.0)
    probs = weights / jnp.sum(weights, axis=(2, 3), keepdims=True)
    probs_low = probs.astype(jnp.bfloat16)
    attended = contract("bijm,bjmd->bid", probs_low, v_sel, False)
    delta = jnp.sum(g_blk.astype(jnp.float32) * attended, axis=2)
    dprobs = contract("bid,bjmd->bijm", g_blk, v_sel, False)
    dscores = (probs * (dprobs - delta[:, :, None, None])).astype(jnp.bfloat16)
    q_grad = (contract("bijm,bjmd->bid", dscores, k_sel, False) * scale).astype(jnp.bfloat16)
    k_slot = contract("bijm,bid->bjmd", dscores, q_blk, False) * scale
    v_slot = contract("bijm,bid->bjmd", probs_low, g_blk, False)
    spread = chosen.astype(jnp.float32)
    k_grad = contract("bjc,bjmd->cmd", spread, k_slot, True).astype(jnp.bfloat16)
    v_grad = contract("bjc,bjmd->cmd", spread, v_slot, True).astype(jnp.bfloat16)
    return (
        q_grad.reshape(tokens, head_dim),
        k_grad.reshape(tokens, head_dim),
        v_grad.reshape(tokens, head_dim),
    )


def heads_attention(query, key_rows, value, grad, ids, blist, head_dim, block):
    tokens, width = query.shape
    heads = width // head_dim

    def split(array):
        return array.reshape(tokens, heads, head_dim).transpose(1, 0, 2)

    def join(array):
        return array.transpose(1, 0, 2).reshape(tokens, width)

    def one_head(item):
        return block_attention(item[0], item[1], item[2], item[3], ids, blist, block)

    q_grad, k_grad, v_grad = lax.map(
        one_head, (split(query), split(key_rows), split(value), split(grad))
    )
    return (join(q_grad), join(k_grad), join(v_grad))


def per_device(queries, keys, events, out_grad, segment_ids, block_list, conv_weight):
    query = queries[0]
    key_rows = keys[0]
    feats = events[0]
    grad = out_grad[0]
    blist = block_list[0]
    rows, width = query.shape
    taps = conv_weight.shape[0]
    shards = lax.axis_size("dp") * lax.axis_size("seq")
    position = lax.axis_index("seq")
    all_ids = lax.all_gather(segment_ids, "seq", axis=1, tiled=True)[0]
    rim = jnp.zeros((taps - 1,), jnp.int32)
    ids_all = jnp.concatenate([rim, all_ids + 1, rim])
    left_ids = lax.dynamic_slice_in_dim(ids_all, position * rows, rows + taps - 1, 0)
    right_ids = lax.dynamic_slice_in_dim(ids_all, position * rows + taps - 1, rows + taps - 1, 0)
    earlier = shifted(feats[rows - (taps - 1) :], "seq", 1)
    padded = jnp.concatenate([earlier, feats], axis=0)
    values = causal_conv(padded, left_ids, conv_weight, rows).astype(jnp.bfloat16)
    head_q, head_k, head_v, head_g = (
        lax.all_to_all(query, "seq", split_axis=1, concat_axis=0, tiled=True),
        lax.all_to_all(key_rows, "seq", split_axis=1, concat_axis=0, tiled=True),
        lax.all_to_all(values, "seq", split_axis=1, concat_axis=0, tiled=True),
        lax.all_to_all(grad, "seq", split_axis=1, concat_axis=0, tiled=True),
    )
    q_grad, k_grad, v_grad = heads_attention(
        head_q, head_k, head_v, head_g, all_ids, blist, HD, BLOCK
    )
    q_back, k_back, v_back = (
        lax.all_to_all(q_grad, "seq", split_axis=0, concat_axis=1, tiled=True),
        lax.all_to_all(k_grad, "seq", split_axis=0, concat_axis=1, tiled=True),
        lax.all_to_all(v_grad, "seq", split_axis=0, concat_axis=1, tiled=True),
    )
    later = shifted(v_back[: taps - 1], "seq", -1)
    after = jnp.concatenate([v_back, later], axis=0)
    e_grad = anti_conv(after, right_ids, conv_weight, rows).astype(jnp.bfloat16)
    f_local = tap_gradient(v_back, padded, left_ids, taps)
    f_grad = lax.psum(f_local, ("dp", "seq")) / shards
    return (q_back[None], k_back[None], e_grad[None], f_grad)


def solution(mesh):
    in_specs = (
        P("dp", "seq", None),
        P("dp", "seq", None),
        P("dp", "seq", None),
        P("dp", "seq", None),
        P("dp", "seq"),
        P("dp", None, None),
        P(),
    )
    out_specs = (P("dp", "seq", None), P("dp", "seq", None), P("dp", "seq", None), P())
    return jax.shard_map(
        per_device, mesh=mesh, in_specs=in_specs, out_specs=out_specs, check_vma=False
    )
```

profile of v0, /device:TPU:1, one launch (start us, length us, event | category | flops | bytes accessed | tf_op | source)
XLA Modules:
  0.0 902.8 jit_solution(13056101979047803530)
XLA Ops:
  9.3 15.7 %all-to-all-start = ((bf16[128,16,128]{0,2,1:T(8,128)(2,1)}), bf16[128,16,128]{0,2,1:T(8,128)(2,1)S(1)}, u32[]{:S(2)}, u32[]{:S(2)}) async-start(bf16[128,16,128]{0,2,1:T(8,128)(2,1)} %bitcast.18), calls=%async_computation | async-start | bytes 1048576 | tf_op jit(solution)/shard_map/all_to_all | solution.py:151
  27.4 3.3 collective-permute-start
  31.7 46.4 %all_gather.3 = s32[1,2048]{1,0:T(1,128)S(1)} all-gather(s32[1,128]{1,0:T(1,128)S(1)} %copy-done.122), channel_id=1, replica_groups=mesh['dp'=32,'seq'=16] {'seq'}, dimensions={1}, use_global_device_ids=true | all-gather | bytes 8704 | tf_op jit(solution)/shard_map/all_gather | solution.py:142
  81.1 8.9 all-to-all-start.1
  95.5 13.0 %all-to-all-done.1 = bf16[128,16,128]{0,2,1:T(8,128)(2,1)S(1)} async-done(((bf16[128,16,128]{0,2,1:T(8,128)(2,1)}), bf16[128,16,128]{0,2,1:T(8,128)(2,1)S(1)}, u32[]{:S(2)}, u32[]{:S(2)}) %all-to-all-start.1) | async-done | bytes 524320 | tf_op jit(solution)/shard_map/all_to_all | solution.py:152
  108.4 13.7 %all-to-all-start.2 = ((bf16[128,16,128]{0,2,1:T(8,128)(2,1)}), bf16[128,16,128]{0,2,1:T(8,128)(2,1)S(1)}, u32[]{:S(2)}, u32[]{:S(2)}) async-start(bf16[128,16,128]{0,2,1:T(8,128)(2,1)} %bitcast.24), calls=%async_computation.2 | async-start | bytes 1048576 | tf_op jit(solution)/shard_map/all_to_all | solution.py:154
  122.1 40.2 %fusion.322 = bf16[128,2048]{0,1:T(8,128)(2,1)S(1)} fusion(bf16[128,2048]{0,1:T(8,128)(2,1)S(1)} %bitcast.375, f32[2048]{0:T(1024)S(1)} %bitcast.429, f32[2048]{0:T(1024)S(1)} %bitcast.431, f32[2048]{0:T(1024)S(1)} %bitcast.435, f32[2048]{0:T(1024)S(1)} %bitcast.437, f32[2048]{0:T(1024)S(1)} %bitcast.439, f32[2048]{0:T(1024)S(1)} %bitcast.441, ...), kind=kLoop, calls=%fused_computation.710 | loop fusion | flops 116391936 | bytes 1838976 | tf_op jit(solution)/shard_map/convert_element_type | solution.py:149
  163.3 11.5 %all-to-all-start.3 = ((bf16[128,16,128]{2,0,1:T(8,128)(2,1)}), bf16[128,16,128]{2,0,1:T(8,128)(2,1)S(1)}, u32[]{:S(2)}, u32[]{:S(2)}) async-start(bf16[128,16,128]{2,0,1:T(8,128)(2,1)} %copy.195), calls=%async_computation.3 | async-start | bytes 1048576 | tf_op jit(solution)/shard_map/all_to_all | solution.py:153
  182.4 12.1 %all-to-all-done.3 = bf16[128,16,128]{2,0,1:T(8,128)(2,1)S(1)} async-done(((bf16[128,16,128]{2,0,1:T(8,128)(2,1)}), bf16[128,16,128]{2,0,1:T(8,128)(2,1)S(1)}, u32[]{:S(2)}, u32[]{:S(2)}) %all-to-all-start.3) | async-done | bytes 524320 | tf_op jit(solution)/shard_map/all_to_all | solution.py:153
  196.0 67.1 %while.18 = (s32[]{:T(128)}, bf16[2,2048,64]{1,2,0:T(8,128)(2,1)}, bf16[2,2048,64]{1,2,0:T(8,128)(2,1)}, bf16[2,2048,64]{1,2,0:T(8,128)(2,1)}, pred[16,4]{1,0:T(...) while((s32[]{:T(128)}, bf16[2,2048,64]{1,2,0:T(8,128)(2,1)}, ...), condition=%wide.region_6.7_spmd, body=%wide.region_1.6_spmd.sunk | while | flops 1074403328 | bytes 83230208 | solution.py:126
  198.6 4.9 fusion.503
  232.0 4.9 fusion.503
  256.8 3.1 fusion.509
  265.3 14.0 %all-to-all-start.4 = ((bf16[16,128,128]{1,2,0:T(8,128)(2,1)}), bf16[16,128,128]{1,2,0:T(8,128)(2,1)S(1)}, u32[]{:S(2)}, u32[]{:S(2)}) async-start(bf16[16,128,128]{1,2,0:T(8,128)(2,1)} %copy.198), calls=%async_computation.4 | async-start | bytes 1048576 | tf_op jit(solution)/shard_map/all_to_all | solution.py:160
  281.7 19.0 %all-to-all-done.4 = bf16[16,128,128]{1,2,0:T(8,128)(2,1)S(1)} async-done(((bf16[16,128,128]{1,2,0:T(8,128)(2,1)}), bf16[16,128,128]{1,2,0:T(8,128)(2,1)S(1)}, u32[]{:S(2)}, u32[]{:S(2)}) %all-to-all-start.4) | async-done | bytes 524320 | tf_op jit(solution)/shard_map/all_to_all | solution.py:160
  300.7 22.1 %all-to-all-start.5 = ((bf16[16,128,128]{2,1,0:T(8,128)(2,1)}), bf16[16,128,128]{2,1,0:T(8,128)(2,1)S(1)}, u32[]{:S(2)}, u32[]{:S(2)}) async-start(bf16[16,128,128]{2,1,0:T(8,128)(2,1)} %copy.199), calls=%async_computation.5 | async-start | bytes 1048576 | tf_op jit(solution)/shard_map/all_to_all | solution.py:161
  324.3 21.0 %all-to-all-done.5 = bf16[16,128,128]{2,1,0:T(8,128)(2,1)S(1)} async-done(((bf16[16,128,128]{2,1,0:T(8,128)(2,1)}), bf16[16,128,128]{2,1,0:T(8,128)(2,1)S(1)}, u32[]{:S(2)}, u32[]{:S(2)}) %all-to-all-start.5) | async-done | bytes 524320 | tf_op jit(solution)/shard_map/all_to_all | solution.py:161
  345.3 12.5 %all-to-all-start.6 = ((bf16[16,128,128]{2,1,0:T(8,128)(2,1)}), bf16[16,128,128]{2,1,0:T(8,128)(2,1)S(1)}, u32[]{:S(2)}, u32[]{:S(2)}) async-start(bf16[16,128,128]{2,1,0:T(8,128)(2,1)} %copy.201), calls=%async_computation.6 | async-start | bytes 1048576 | tf_op jit(solution)/shard_map/all_to_all | solution.py:162
  360.9 19.7 %all-to-all-done.6 = bf16[16,128,128]{2,1,0:T(8,128)(2,1)S(1)} async-done(((bf16[16,128,128]{2,1,0:T(8,128)(2,1)}), bf16[16,128,128]{2,1,0:T(8,128)(2,1)S(1)}, u32[]{:S(2)}, u32[]{:S(2)}) %all-to-all-start.6) | async-done | bytes 524320 | tf_op jit(solution)/shard_map/all_to_all | solution.py:162
  382.3 3.4 fusion.321
  385.9 3.6 fusion.223
  389.5 4.1 fusion.235
  393.7 3.6 fusion.247
  397.3 3.6 fusion.259
  401.0 3.6 fusion.271
  404.6 3.8 fusion.283
  408.8 4.2 fusion.295
  413.0 4.3 fusion.307
  417.3 4.2 fusion.319
  424.2 5.8 stack.259
  430.5 41.2 %fusion.447 = bf16[1,128,2048]{1,2,0:T(8,128)(2,1)S(1)} fusion(f32[2048]{0:T(1024)S(1)} %bitcast.430, bf16[63,2048]{0,1:T(8,128)(2,1)S(1)} %collective-permute-done.1, bf16[128,2048]{0,1:T(8,128)(2,1)S(1)} %bitcast.391, pred[128]{0:T(512)(128)(4,1)S(1)} %get-tuple-element.460, f32[2048]{0:T(1024)S(1)} %bitcast.432, ...), kind=kLoop, calls=%fused_computation.838 | loop fusion | flops 116391936 | bytes 1838976 | tf_op jit(solution)/shard_map/broadcast_in_dim | solution.py:169
  472.7 420.9 %all-reduce.2.cloned.1.call-done = f32[64,2048]{1,0:T(8,128)} async-done(((f32[64,2048]{1,0:T(8,128)}), f32[64,2048]{1,0:T(8,128)}) %all-reduce.2.cloned.1.call-update) | async-done | bytes 524304 | tf_op jit(solution)/shard_map/psum | solution.py:168
  (382 shorter events, 93.2 us)
Async XLA Ops:
  9.3 71.8 %all-to-all-start = ((bf16[128,16,128]{0,2,1:T(8,128)(2,1)}), bf16[128,16,128]{0,2,1:T(8,128)(2,1)S(1)}, u32[]{:S(2)}, u32[]{:S(2)}) async-start(bf16[128,16,128]{0,2,1:T(8,128)(2,1)} %bitcast.18), calls=%async_computation | async-start | bytes 1048576 | tf_op jit(solution)/shard_map/all_to_all | solution.py:151
  27.4 94.7 %collective-permute-start = (bf16[63,2048]{0,1:T(8,128)(2,1)}, bf16[63,2048]{0,1:T(8,128)(2,1)S(1)}, u32[]{:S(2)}, u32[]{:S(2)}) collective-permute-start(bf16[63,2048]{0,1:T(8,128)(2,1)} %slice_bitcast_fusion), channel_id=1, source_target_pairs={{0,1},{1,2},{2,3},{3,4},{4,5},{5,6},{6,7},{7,8},{8,9},{9,10},{10,1... | collective-permute-start | bytes 774152 | tf_op jit(solution)/shard_map/ppermute | solution.py:13
  81.1 93.7 %copy-start.2 = (s32[1,16,4]{1,2,0:T(4,128)S(1)}, s32[1,16,4]{1,2,0:T(4,128)}, u32[]{:S(2)}) copy-start(s32[1,16,4]{1,2,0:T(4,128)} %param.14) | copy-start | bytes 772
  81.1 27.3 %all-to-all-start.1 = ((bf16[128,16,128]{0,2,1:T(8,128)(2,1)}), bf16[128,16,128]{0,2,1:T(8,128)(2,1)S(1)}, u32[]{:S(2)}, u32[]{:S(2)}) async-start(bf16[128,16,128]{0,2,1:T(8,128)(2,1)} %bitcast.21), calls=%async_computation.1 | async-start | bytes 1048576 | tf_op jit(solution)/shard_map/all_to_all | solution.py:152
  91.1 88.4 %copy-start.30 = (f32[1,2048]{1,0:T(1,128)}, f32[1,2048]{1,0:T(1,128)S(1)}, u32[]{:S(2)}) copy-start(f32[1,2048]{1,0:T(1,128)S(1)} %get-tuple-element.351) | copy-start | bytes 24580
  91.1 88.4 %copy-start.32 = (f32[1,2048]{1,0:T(1,128)}, f32[1,2048]{1,0:T(1,128)S(1)}, u32[]{:S(2)}) copy-start(f32[1,2048]{1,0:T(1,128)S(1)} %get-tuple-element.352) | copy-start | bytes 24580
  91.1 88.4 %copy-start.34 = (f32[1,2048]{1,0:T(1,128)}, f32[1,2048]{1,0:T(1,128)S(1)}, u32[]{:S(2)}) copy-start(f32[1,2048]{1,0:T(1,128)S(1)} %get-tuple-element.353) | copy-start | bytes 24580
  91.1 88.4 %copy-start.36 = (f32[1,2048]{1,0:T(1,128)}, f32[1,2048]{1,0:T(1,128)S(1)}, u32[]{:S(2)}) copy-start(f32[1,2048]{1,0:T(1,128)S(1)} %get-tuple-element.354) | copy-start | bytes 24580
  91.1 88.4 %copy-start.38 = (f32[1,2048]{1,0:T(1,128)}, f32[1,2048]{1,0:T(1,128)S(1)}, u32[]{:S(2)}) copy-start(f32[1,2048]{1,0:T(1,128)S(1)} %get-tuple-element.355) | copy-start | bytes 24580
  91.1 88.4 %copy-start.40 = (f32[1,2048]{1,0:T(1,128)}, f32[1,2048]{1,0:T(1,128)S(1)}, u32[]{:S(2)}) copy-start(f32[1,2048]{1,0:T(1,128)S(1)} %get-tuple-element.356) | copy-start | bytes 24580
  91.1 88.4 %copy-start.42 = (f32[1,2048]{1,0:T(1,128)}, f32[1,2048]{1,0:T(1,128)S(1)}, u32[]{:S(2)}) copy-start(f32[1,2048]{1,0:T(1,128)S(1)} %get-tuple-element.357) | copy-start | bytes 24580
  91.2 88.4 %copy-start.44 = (f32[1,2048]{1,0:T(1,128)}, f32[1,2048]{1,0:T(1,128)S(1)}, u32[]{:S(2)}) copy-start(f32[1,2048]{1,0:T(1,128)S(1)} %get-tuple-element.358) | copy-start | bytes 24580
  91.2 88.4 %copy-start.46 = (f32[1,2048]{1,0:T(1,128)}, f32[1,2048]{1,0:T(1,128)S(1)}, u32[]{:S(2)}) copy-start(f32[1,2048]{1,0:T(1,128)S(1)} %get-tuple-element.359) | copy-start | bytes 24580
  91.2 88.4 %copy-start.48 = (f32[1,2048]{1,0:T(1,128)}, f32[1,2048]{1,0:T(1,128)S(1)}, u32[]{:S(2)}) copy-start(f32[1,2048]{1,0:T(1,128)S(1)} %get-tuple-element.360) | copy-start | bytes 24580
  91.2 88.4 %copy-start.50 = (f32[1,2048]{1,0:T(1,128)}, f32[1,2048]{1,0:T(1,128)S(1)}, u32[]{:S(2)}) copy-start(f32[1,2048]{1,0:T(1,128)S(1)} %get-tuple-element.361) | copy-start | bytes 24580
  91.2 88.4 %copy-start.52 = (f32[1,2048]{1,0:T(1,128)}, f32[1,2048]{1,0:T(1,128)S(1)}, u32[]{:S(2)}) copy-start(f32[1,2048]{1,0:T(1,128)S(1)} %get-tuple-element.362) | copy-start | bytes 24580
  91.2 88.4 %copy-start.54 = (f32[1,2048]{1,0:T(1,128)}, f32[1,2048]{1,0:T(1,128)S(1)}, u32[]{:S(2)}) copy-start(f32[1,2048]{1,0:T(1,128)S(1)} %get-tuple-element.363) | copy-start | bytes 24580
  91.2 88.4 %copy-start.56 = (f32[1,2048]{1,0:T(1,128)}, f32[1,2048]{1,0:T(1,128)S(1)}, u32[]{:S(2)}) copy-start(f32[1,2048]{1,0:T(1,128)S(1)} %get-tuple-element.364) | copy-start | bytes 24580
  91.2 88.4 %copy-start.58 = (f32[1,2048]{1,0:T(1,128)}, f32[1,2048]{1,0:T(1,128)S(1)}, u32[]{:S(2)}) copy-start(f32[1,2048]{1,0:T(1,128)S(1)} %get-tuple-element.365) | copy-start | bytes 24580
  108.4 54.9 %all-to-all-start.2 = ((bf16[128,16,128]{0,2,1:T(8,128)(2,1)}), bf16[128,16,128]{0,2,1:T(8,128)(2,1)S(1)}, u32[]{:S(2)}, u32[]{:S(2)}) async-start(bf16[128,16,128]{0,2,1:T(8,128)(2,1)} %bitcast.24), calls=%async_computation.2 | async-start | bytes 1048576 | tf_op jit(solution)/shard_map/all_to_all | solution.py:154
  163.3 31.2 %all-to-all-start.3 = ((bf16[128,16,128]{2,0,1:T(8,128)(2,1)}), bf16[128,16,128]{2,0,1:T(8,128)(2,1)S(1)}, u32[]{:S(2)}, u32[]{:S(2)}) async-start(bf16[128,16,128]{2,0,1:T(8,128)(2,1)} %copy.195), calls=%async_computation.3 | async-start | bytes 1048576 | tf_op jit(solution)/shard_map/all_to_all | solution.py:153
  265.3 35.5 %all-to-all-start.4 = ((bf16[16,128,128]{1,2,0:T(8,128)(2,1)}), bf16[16,128,128]{1,2,0:T(8,128)(2,1)S(1)}, u32[]{:S(2)}, u32[]{:S(2)}) async-start(bf16[16,128,128]{1,2,0:T(8,128)(2,1)} %copy.198), calls=%async_computation.4 | async-start | bytes 1048576 | tf_op jit(solution)/shard_map/all_to_all | solution.py:160
  281.7 100.6 %copy-start.99 = (pred[128]{0:T(512)(128)(4,1)S(1)}, pred[128]{0:T(512)(128)(4,1)}, u32[]{:S(2)}) copy-start(pred[128]{0:T(512)(128)(4,1)} %get-tuple-element.523) | copy-start | bytes 388
  281.7 100.6 %copy-start.102 = (pred[128]{0:T(512)(128)(4,1)S(1)}, pred[128]{0:T(512)(128)(4,1)}, u32[]{:S(2)}) copy-start(pred[128]{0:T(512)(128)(4,1)} %get-tuple-element.461) | copy-start | bytes 388
  281.7 100.6 %copy-start.103 = (pred[128]{0:T(512)(128)(4,1)S(1)}, pred[128]{0:T(512)(128)(4,1)}, u32[]{:S(2)}) copy-start(pred[128]{0:T(512)(128)(4,1)} %get-tuple-element.470) | copy-start | bytes 388
  281.7 100.6 %copy-start.104 = (pred[128]{0:T(512)(128)(4,1)S(1)}, pred[128]{0:T(512)(128)(4,1)}, u32[]{:S(2)}) copy-start(pred[128]{0:T(512)(128)(4,1)} %get-tuple-element.479) | copy-start | bytes 388
  281.7 100.6 %copy-start.105 = (pred[128]{0:T(512)(128)(4,1)S(1)}, pred[128]{0:T(512)(128)(4,1)}, u32[]{:S(2)}) copy-start(pred[128]{0:T(512)(128)(4,1)} %get-tuple-element.488) | copy-start | bytes 388
  281.7 100.6 %copy-start.121 = (pred[128]{0:T(512)(128)(4,1)S(1)}, pred[128]{0:T(512)(128)(4,1)}, u32[]{:S(2)}) copy-start(pred[128]{0:T(512)(128)(4,1)} %get-tuple-element.497) | copy-start | bytes 388
  300.7 44.6 %all-to-all-start.5 = ((bf16[16,128,128]{2,1,0:T(8,128)(2,1)}), bf16[16,128,128]{2,1,0:T(8,128)(2,1)S(1)}, u32[]{:S(2)}, u32[]{:S(2)}) async-start(bf16[16,128,128]{2,1,0:T(8,128)(2,1)} %copy.199), calls=%async_computation.5 | async-start | bytes 1048576 | tf_op jit(solution)/shard_map/all_to_all | solution.py:161
  345.3 35.3 %all-to-all-start.6 = ((bf16[16,128,128]{2,1,0:T(8,128)(2,1)}), bf16[16,128,128]{2,1,0:T(8,128)(2,1)S(1)}, u32[]{:S(2)}, u32[]{:S(2)}) async-start(bf16[16,128,128]{2,1,0:T(8,128)(2,1)} %copy.201), calls=%async_computation.6 | async-start | bytes 1048576 | tf_op jit(solution)/shard_map/all_to_all | solution.py:162
  357.8 535.8 %all-reduce.2.cloned.1.call-start = ((), (), s32[]{:S(2)}) async-start(), calls=%async_computation.7 | async-start | bytes 1048576 | tf_op jit(solution)/shard_map/psum | solution.py:168
  381.0 49.1 %collective-permute-start.1 = (bf16[63,2048]{0,1:T(8,128)(2,1)S(1)}, bf16[63,2048]{0,1:T(8,128)(2,1)S(1)}, u32[]{:S(2)}, u32[]{:S(2)}) collective-permute-start(bf16[63,2048]{0,1:T(8,128)(2,1)S(1)} %bitcast.390), channel_id=1, source_target_pairs={{1,0},{2,1},{3,2},{4,3},{5,4},{6,5},{7,6},{8,7},{9,8},{10,9},{11,1... | collective-permute-start | bytes 774152 | tf_op jit(solution)/shard_map/ppermute | solution.py:13
  (105 other events, 4006.6 us)
Sparse Core Ops, SparseCore 0:
  430.2 463.4 all-reduce.1
where the time goes:
time: 913 us; the launch traced here: 903 us
  waiting for transfers between devices  506 us (55%)
  other arithmetic  143 us (16%)
  starting transfers between devices  103 us (11%)
  local copies, waits for them, and re-layouts  51.7 us (6%)
  blocking collectives  46.4 us (5%)
  matrix products  35.5 us (4%)
  between operations  16.6 us (2%)
    psum x1, waiting for transfers between devices, per_device(): f_grad = lax.psum(f_local, ('dp', 'seq')) / shards  421 us
    all_gather x1, blocking collectives, per_device(): all_ids = lax.all_gather(segment_ids, 'seq', axis=1, tiled=True)[0]  46.4 us
    broadcast_in_dim x1, other arithmetic, per_device(): return (q_back[None], k_back[None], e_grad[None], f_grad)  41.2 us
    reduce_sum x11, other arithmetic, tap_gradient(): sums.append(jnp.sum(jnp.where(match, piece * grad_wide, 0.0), axis=0))  41 us
    convert_element_type x1, other arithmetic, per_device(): causal_conv(padded, left_ids, conv_weight, rows).astype(jnp.bfloat16)  40.2 us
    dot_general x16, matrix products, contract(): return jnp.einsum(form, left, right, preferred_element_type=jnp.float32)  26.3 us
    all_to_all x1, starting transfers between devices, per_device(): lax.all_to_all(k_grad, 'seq', split_axis=0, concat_axis=1, tiled=True)  22.1 us
    all_to_all x1, waiting for transfers between devices, per_device(): lax.all_to_all(k_grad, 'seq', split_axis=0, concat_axis=1, tiled=True)  21 us
  transfers between devices with their start and end apart: 10, of which 6 were waited for; matrix products, arithmetic and copies ran while one was open for 17% of the time, Pallas kernels for 0%

commit v1 on v0

--- a/solution.py
+++ b/solution.py
@@ -1,7 +1,11 @@
 import jax
 import jax.numpy as jnp
 from jax import lax
+from jax.experimental import pallas as pl
+from jax.experimental.pallas import tpu as pltpu
 from jax.sharding import PartitionSpec as P
+
+MESH = pl.DeviceIdType.MESH
 
 HD = 64
 BLOCK = 128
@@ -129,6 +133,137 @@
     return (join(q_grad), join(k_grad), join(v_grad))
 
 
+def spread_sum(local, scale):
+    n_dp, n_seq = lax.axis_size("dp"), lax.axis_size("seq")
+    taps, width = local.shape
+    lanes = 128
+    parts = width // lanes
+    split = n_dp // parts
+    rows = taps // split
+
+    def kernel(x_ref, o_ref, mine, got, part, gotz, tot, done, s1, r1, s2, r2, s3, r3):
+        me = lax.axis_index("dp")
+        z = lax.axis_index("seq")
+        barrier = pltpu.get_barrier_semaphore()
+
+        def greet_dp(i, _):
+            pl.semaphore_signal(barrier, inc=1, device_id={"dp": lax.rem(me + i, n_dp)}, device_id_type=MESH)
+            return 0
+
+        def greet_z(i, _):
+            pl.semaphore_signal(barrier, inc=1, device_id={"seq": lax.rem(z + i, n_seq)}, device_id_type=MESH)
+            return 0
+
+        lax.fori_loop(1, n_dp, greet_dp, 0)
+        lax.fori_loop(1, n_seq, greet_z, 0)
+        for j in range(n_dp):
+            col, row = (j // split) * lanes, (j % split) * rows
+            mine[j] = x_ref[row : row + rows, col : col + lanes].astype(jnp.bfloat16)
+        pl.semaphore_wait(barrier, n_dp + n_seq - 2)
+
+        def out1(i):
+            to = lax.rem(me + i, n_dp)
+            return pltpu.make_async_remote_copy(
+                src_ref=mine.at[to], dst_ref=got.at[me], send_sem=s1.at[i], recv_sem=r1.at[me],
+                device_id={"dp": to}, device_id_type=MESH)
+
+        def in1(i):
+            src = lax.rem(me + i, n_dp)
+            return pltpu.make_async_remote_copy(
+                src_ref=mine.at[src], dst_ref=got.at[src], send_sem=s1.at[i], recv_sem=r1.at[src],
+                device_id={"dp": src}, device_id_type=MESH)
+
+        def out2(i):
+            to = lax.rem(z + i, n_seq)
+            return pltpu.make_async_remote_copy(
+                src_ref=part, dst_ref=gotz.at[z], send_sem=s2.at[i], recv_sem=r2.at[z],
+                device_id={"seq": to}, device_id_type=MESH)
+
+        def in2(i):
+            src = lax.rem(z + i, n_seq)
+            return pltpu.make_async_remote_copy(
+                src_ref=part, dst_ref=gotz.at[src], send_sem=s2.at[i], recv_sem=r2.at[src],
+                device_id={"seq": src}, device_id_type=MESH)
+
+        def out3(i):
+            to = lax.rem(me + i, n_dp)
+            return pltpu.make_async_remote_copy(
+                src_ref=tot, dst_ref=done.at[me], send_sem=s3.at[i], recv_sem=r3.at[me],
+                device_id={"dp": to}, device_id_type=MESH)
+
+        def in3(i):
+            src = lax.rem(me + i, n_dp)
+            return pltpu.make_async_remote_copy(
+                src_ref=tot, dst_ref=done.at[src], send_sem=s3.at[i], recv_sem=r3.at[src],
+                device_id={"dp": src}, device_id_type=MESH)
+
+        def start(make, count):
+            def body(i, _):
+                make(i).start()
+                return 0
+            lax.fori_loop(1, count, body, 0)
+
+        def sent(make, count):
+            def body(i, _):
+                make(i).wait_send()
+                return 0
+            lax.fori_loop(1, count, body, 0)
+
+        def landed(make, count):
+            def body(i, _):
+                make(i).wait_recv()
+                return 0
+            lax.fori_loop(1, count, body, 0)
+
+        start(out1, n_dp)
+        got[me] = mine[me]
+        landed(in1, n_dp)
+        total = got[0].astype(jnp.float32)
+        for j in range(1, n_dp):
+            total = total + got[j].astype(jnp.float32)
+        part[...] = total.astype(jnp.bfloat16)
+        start(out2, n_seq)
+        gotz[z] = part[...]
+        landed(in2, n_seq)
+        total = gotz[0].astype(jnp.float32)
+        for j in range(1, n_seq):
+            total = total + gotz[j].astype(jnp.float32)
+        tot[...] = (total * scale).astype(jnp.bfloat16)
+        start(out3, n_dp)
+        done[me] = tot[...]
+        landed(in3, n_dp)
+        for j in range(n_dp):
+            col, row = (j // split) * lanes, (j % split) * rows
+            o_ref[row : row + rows, col : col + lanes] = done[j].astype(jnp.float32)
+        sent(out1, n_dp)
+        sent(out2, n_seq)
+        sent(out3, n_dp)
+
+    piece = (rows, lanes)
+    return pl.pallas_call(
+        kernel,
+        out_shape=jax.ShapeDtypeStruct((taps, width), jnp.float32),
+        in_specs=[pl.BlockSpec(memory_space=pltpu.VMEM)],
+        out_specs=pl.BlockSpec(memory_space=pltpu.VMEM),
+        scratch_shapes=[
+            pltpu.VMEM((n_dp,) + piece, jnp.bfloat16),
+            pltpu.VMEM((n_dp,) + piece, jnp.bfloat16),
+            pltpu.VMEM(piece, jnp.bfloat16),
+            pltpu.VMEM((n_seq,) + piece, jnp.bfloat16),
+            pltpu.VMEM(piece, jnp.bfloat16),
+            pltpu.VMEM((n_dp,) + piece, jnp.bfloat16),
+            pltpu.SemaphoreType.DMA((n_dp,)),
+            pltpu.SemaphoreType.DMA((n_dp,)),
+            pltpu.SemaphoreType.DMA((n_seq,)),
+            pltpu.SemaphoreType.DMA((n_seq,)),
+            pltpu.SemaphoreType.DMA((n_dp,)),
+            pltpu.SemaphoreType.DMA((n_dp,)),
+        ],
+        compiler_params=pltpu.CompilerParams(collective_id=1, has_side_effects=True),
+        name="spread_sum",
+    )(local)
+
+
 def per_device(queries, keys, events, out_grad, segment_ids, block_list, conv_weight):
     query = queries[0]
     key_rows = keys[0]
@@ -165,7 +300,7 @@
     after = jnp.concatenate([v_back, later], axis=0)
     e_grad = anti_conv(after, right_ids, conv_weight, rows).astype(jnp.bfloat16)
     f_local = tap_gradient(v_back, padded, left_ids, taps)
-    f_grad = lax.psum(f_local, ("dp", "seq")) / shards
+    f_grad = spread_sum(f_local, 1.0 / shards)
     return (q_back[None], k_back[None], e_grad[None], f_grad)
 
 

time: 913 us -> 520 us (0.57)
  waiting for transfers between devices: 506 us -> 84.9 us
  Pallas kernels: 0 us -> 41.7 us
  between operations: 16.6 us -> 3.2 us
    psum x1 -> x0, waiting for transfers between devices: 421 us -> none  [per_device(): f_grad = lax.psum(f_local, ('dp', 'seq')) / shards]
    pallas_call x0 -> x1, Pallas kernels: none -> 41.7 us  [spread_sum(): pl.pallas_call(kernel, out_shape=jax.ShapeDtypeStruct((taps, width), jnp....]
  transfers between devices with their start and end apart: 10 -> 9, of which waited for: 6 -> 5; matrix products, arithmetic and copies ran while one was open for 17% -> 22% of each run, Pallas kernels for 0% -> 8%
where the time goes in v1:
time: 520 us; the launch traced here: 510 us
  other arithmetic  141 us (27%)
  starting transfers between devices  103 us (20%)
  waiting for transfers between devices  84.9 us (16%)
  local copies, waits for them, and re-layouts  53.6 us (10%)
  blocking collectives  46.4 us (9%)
  Pallas kernels  41.7 us (8%)
  matrix products  35.5 us (7%)
    all_gather x1, blocking collectives, per_device(): all_ids = lax.all_gather(segment_ids, 'seq', axis=1, tiled=True)[0]  46.4 us
    pallas_call x1, Pallas kernels, spread_sum(): pl.pallas_call(kernel, out_shape=jax.ShapeDtypeStruct((taps, width), jnp....  41.7 us
    broadcast_in_dim x1, other arithmetic, per_device(): return (q_back[None], k_back[None], e_grad[None], f_grad)  41.2 us
    reduce_sum x11, other arithmetic, tap_gradient(): sums.append(jnp.sum(jnp.where(match, piece * grad_wide, 0.0), axis=0))  41.1 us
    convert_element_type x1, other arithmetic, per_device(): causal_conv(padded, left_ids, conv_weight, rows).astype(jnp.bfloat16)  40.2 us
    dot_general x16, matrix products, contract(): return jnp.einsum(form, left, right, preferred_element_type=jnp.float32)  26.3 us
    all_to_all x1, starting transfers between devices, per_device(): lax.all_to_all(k_grad, 'seq', split_axis=0, concat_axis=1, tiled=True)  22.1 us
    all_to_all x1, waiting for transfers between devices, per_device(): lax.all_to_all(k_grad, 'seq', split_axis=0, concat_axis=1, tiled=True)  21 us
  transfers between devices with their start and end apart: 9, of which 5 were waited for; matrix products, arithmetic and copies ran while one was open for 22% of the time, Pallas kernels for 8%

profile of v1, /device:TPU:1, one launch (start us, length us, event | category | flops | bytes accessed | tf_op | source)
XLA Modules:
  0.0 510.3 jit_solution(9216494127682115917)
XLA Ops:
  2.8 15.7 %all-to-all-start = ((bf16[128,16,128]{0,2,1:T(8,128)(2,1)}), bf16[128,16,128]{0,2,1:T(8,128)(2,1)S(1)}, u32[]{:S(2)}, u32[]{:S(2)}) async-start(bf16[128,16,128]{0,2,1:T(8,128)(2,1)} %bitcast.18), calls=%async_computation | async-start | bytes 1048576 | tf_op jit(solution)/shard_map/all_to_all | solution.py:286
  20.9 3.3 collective-permute-start
  25.2 46.4 %all_gather.3 = s32[1,2048]{1,0:T(1,128)S(1)} all-gather(s32[1,128]{1,0:T(1,128)S(1)} %copy-done.122), channel_id=1, replica_groups=mesh['dp'=32,'seq'=16] {'seq'}, dimensions={1}, use_global_device_ids=true | all-gather | bytes 8704 | tf_op jit(solution)/shard_map/all_gather | solution.py:277
  74.6 8.9 %all-to-all-start.1 = ((bf16[128,16,128]{0,2,1:T(8,128)(2,1)}), bf16[128,16,128]{0,2,1:T(8,128)(2,1)S(1)}, u32[]{:S(2)}, u32[]{:S(2)}) async-start(bf16[128,16,128]{0,2,1:T(8,128)(2,1)} %bitcast.21), calls=%async_computation.1 | async-start | bytes 1048576 | tf_op jit(solution)/shard_map/all_to_all | solution.py:287
  88.9 13.0 %all-to-all-done.1 = bf16[128,16,128]{0,2,1:T(8,128)(2,1)S(1)} async-done(((bf16[128,16,128]{0,2,1:T(8,128)(2,1)}), bf16[128,16,128]{0,2,1:T(8,128)(2,1)S(1)}, u32[]{:S(2)}, u32[]{:S(2)}) %all-to-all-start.1) | async-done | bytes 524320 | tf_op jit(solution)/shard_map/all_to_all | solution.py:287
  101.9 13.7 %all-to-all-start.2 = ((bf16[128,16,128]{0,2,1:T(8,128)(2,1)}), bf16[128,16,128]{0,2,1:T(8,128)(2,1)S(1)}, u32[]{:S(2)}, u32[]{:S(2)}) async-start(bf16[128,16,128]{0,2,1:T(8,128)(2,1)} %bitcast.24), calls=%async_computation.2 | async-start | bytes 1048576 | tf_op jit(solution)/shard_map/all_to_all | solution.py:289
  115.6 40.2 %fusion.322 = bf16[128,2048]{0,1:T(8,128)(2,1)S(1)} fusion(bf16[128,2048]{0,1:T(8,128)(2,1)S(1)} %bitcast.375, f32[2048]{0:T(1024)S(1)} %bitcast.429, f32[2048]{0:T(1024)S(1)} %bitcast.431, f32[2048]{0:T(1024)S(1)} %bitcast.435, f32[2048]{0:T(1024)S(1)} %bitcast.437, f32[2048]{0:T(1024)S(1)} %bitcast.439, f32[2048]{0:T(1024)S(1)} %bitcast.441, ...), kind=kLoop, calls=%fused_computation.710 | loop fusion | flops 116391936 | bytes 1838976 | tf_op jit(solution)/shard_map/convert_element_type | solution.py:284
  156.8 11.5 %all-to-all-start.3 = ((bf16[128,16,128]{2,0,1:T(8,128)(2,1)}), bf16[128,16,128]{2,0,1:T(8,128)(2,1)S(1)}, u32[]{:S(2)}, u32[]{:S(2)}) async-start(bf16[128,16,128]{2,0,1:T(8,128)(2,1)} %copy.195), calls=%async_computation.3 | async-start | bytes 1048576 | tf_op jit(solution)/shard_map/all_to_all | solution.py:288
  175.9 12.1 %all-to-all-done.3 = bf16[128,16,128]{2,0,1:T(8,128)(2,1)S(1)} async-done(((bf16[128,16,128]{2,0,1:T(8,128)(2,1)}), bf16[128,16,128]{2,0,1:T(8,128)(2,1)S(1)}, u32[]{:S(2)}, u32[]{:S(2)}) %all-to-all-start.3) | async-done | bytes 524320 | tf_op jit(solution)/shard_map/all_to_all | solution.py:288
  189.4 67.1 %while.18 = (s32[]{:T(128)}, bf16[2,2048,64]{1,2,0:T(8,128)(2,1)}, bf16[2,2048,64]{1,2,0:T(8,128)(2,1)}, bf16[2,2048,64]{1,2,0:T(8,128)(2,1)}, pred[16,4]{1,0:T(...) while((s32[]{:T(128)}, bf16[2,2048,64]{1,2,0:T(8,128)(2,1)}, ...), condition=%wide.region_6.7_spmd, body=%wide.region_1.6_spmd.sunk | while | flops 1074403328 | bytes 83230208 | solution.py:130
  192.1 4.9 fusion.503
  225.5 4.9 fusion.503
  250.2 3.1 fusion.509
  258.7 14.0 %all-to-all-start.4 = ((bf16[16,128,128]{1,2,0:T(8,128)(2,1)}), bf16[16,128,128]{1,2,0:T(8,128)(2,1)S(1)}, u32[]{:S(2)}, u32[]{:S(2)}) async-start(bf16[16,128,128]{1,2,0:T(8,128)(2,1)} %copy.198), calls=%async_computation.4 | async-start | bytes 1048576 | tf_op jit(solution)/shard_map/all_to_all | solution.py:295
  275.2 19.0 %all-to-all-done.4 = bf16[16,128,128]{1,2,0:T(8,128)(2,1)S(1)} async-done(((bf16[16,128,128]{1,2,0:T(8,128)(2,1)}), bf16[16,128,128]{1,2,0:T(8,128)(2,1)S(1)}, u32[]{:S(2)}, u32[]{:S(2)}) %all-to-all-start.4) | async-done | bytes 524320 | tf_op jit(solution)/shard_map/all_to_all | solution.py:295
  294.2 22.1 %all-to-all-start.5 = ((bf16[16,128,128]{2,1,0:T(8,128)(2,1)}), bf16[16,128,128]{2,1,0:T(8,128)(2,1)S(1)}, u32[]{:S(2)}, u32[]{:S(2)}) async-start(bf16[16,128,128]{2,1,0:T(8,128)(2,1)} %copy.199), calls=%async_computation.5 | async-start | bytes 1048576 | tf_op jit(solution)/shard_map/all_to_all | solution.py:296
  317.7 21.0 %all-to-all-done.5 = bf16[16,128,128]{2,1,0:T(8,128)(2,1)S(1)} async-done(((bf16[16,128,128]{2,1,0:T(8,128)(2,1)}), bf16[16,128,128]{2,1,0:T(8,128)(2,1)S(1)}, u32[]{:S(2)}, u32[]{:S(2)}) %all-to-all-start.5) | async-done | bytes 524320 | tf_op jit(solution)/shard_map/all_to_all | solution.py:296
  338.7 12.5 %all-to-all-start.6 = ((bf16[16,128,128]{2,1,0:T(8,128)(2,1)}), bf16[16,128,128]{2,1,0:T(8,128)(2,1)S(1)}, u32[]{:S(2)}, u32[]{:S(2)}) async-start(bf16[16,128,128]{2,1,0:T(8,128)(2,1)} %copy.201), calls=%async_computation.6 | async-start | bytes 1048576 | tf_op jit(solution)/shard_map/all_to_all | solution.py:297
  354.3 19.8 %all-to-all-done.6 = bf16[16,128,128]{2,1,0:T(8,128)(2,1)S(1)} async-done(((bf16[16,128,128]{2,1,0:T(8,128)(2,1)}), bf16[16,128,128]{2,1,0:T(8,128)(2,1)S(1)}, u32[]{:S(2)}, u32[]{:S(2)}) %all-to-all-start.6) | async-done | bytes 524320 | tf_op jit(solution)/shard_map/all_to_all | solution.py:297
  375.8 3.4 fusion.321
  379.3 3.6 fusion.223
  383.0 4.2 fusion.235
  387.3 4.2 fusion.247
  391.5 3.6 fusion.259
  395.2 3.6 fusion.271
  398.8 3.8 fusion.283
  402.6 3.6 fusion.295
  406.6 4.3 fusion.307
  410.9 4.2 fusion.319
  417.8 5.8 %stack.259.x_ref = f32[64,2048]{1,0:T(8,128)} concatenate(f32[1,2048]{1,0:T(1,128)S(1)} %bitcast.610, f32[1,2048]{1,0:T(1,128)S(1)} %bitcast.548, f32[1,2048]{1,0:T(1,128)S(1)} %bitcast.549, f32[1,2048]{1,0:T(1,128)S(1)} %bitcast.550, f32[1,2048]{1,0:T(1,128)S(1)} %bitcast.551, f32[1,2048]{1,0:T(1,128)S(1)} %bitcast.552, f32[1,2048]{1,0:T(1,128)S(1)} %bitcast.609, ...), dimensions={0} | concatenate | bytes 1048576 | tf_op jit(solution)/shard_map/stack | solution.py:61
  423.6 41.7 %spread_sum.1 = f32[64,2048]{1,0:T(8,128)} custom-call(f32[64,2048]{1,0:T(8,128)} %stack.259.x_ref), custom_call_target="tpu_custom_call" | custom-call | tf_op jit(solution)/shard_map/spread_sum/pallas_call | solution.py:243
  465.8 41.2 %fusion.447 = bf16[1,128,2048]{1,2,0:T(8,128)(2,1)S(1)} fusion(f32[2048]{0:T(1024)S(1)} %bitcast.430, bf16[63,2048]{0,1:T(8,128)(2,1)S(1)} %collective-permute-done.1, bf16[128,2048]{0,1:T(8,128)(2,1)S(1)} %bitcast.391, pred[128]{0:T(512)(128)(4,1)S(1)} %get-tuple-element.460, f32[2048]{0:T(1024)S(1)} %bitcast.432, ...), kind=kLoop, calls=%fused_computation.838 | loop fusion | flops 116391936 | bytes 1838976 | tf_op jit(solution)/shard_map/broadcast_in_dim | solution.py:304
  (380 shorter events, 93.1 us)
Async XLA Ops:
  2.8 71.8 %all-to-all-start = ((bf16[128,16,128]{0,2,1:T(8,128)(2,1)}), bf16[128,16,128]{0,2,1:T(8,128)(2,1)S(1)}, u32[]{:S(2)}, u32[]{:S(2)}) async-start(bf16[128,16,128]{0,2,1:T(8,128)(2,1)} %bitcast.18), calls=%async_computation | async-start | bytes 1048576 | tf_op jit(solution)/shard_map/all_to_all | solution.py:286
  20.9 94.7 %collective-permute-start = (bf16[63,2048]{0,1:T(8,128)(2,1)}, bf16[63,2048]{0,1:T(8,128)(2,1)S(1)}, u32[]{:S(2)}, u32[]{:S(2)}) collective-permute-start(bf16[63,2048]{0,1:T(8,128)(2,1)} %slice_bitcast_fusion), channel_id=1, source_target_pairs={{0,1},{1,2},{2,3},{3,4},{4,5},{5,6},{6,7},{7,8},{8,9},{9,10},{10,1... | collective-permute-start | bytes 774152 | tf_op jit(solution)/shard_map/ppermute | solution.py:17
  74.6 93.7 %copy-start.2 = (s32[1,16,4]{1,2,0:T(4,128)S(1)}, s32[1,16,4]{1,2,0:T(4,128)}, u32[]{:S(2)}) copy-start(s32[1,16,4]{1,2,0:T(4,128)} %param.14) | copy-start | bytes 772
  74.6 27.3 %all-to-all-start.1 = ((bf16[128,16,128]{0,2,1:T(8,128)(2,1)}), bf16[128,16,128]{0,2,1:T(8,128)(2,1)S(1)}, u32[]{:S(2)}, u32[]{:S(2)}) async-start(bf16[128,16,128]{0,2,1:T(8,128)(2,1)} %bitcast.21), calls=%async_computation.1 | async-start | bytes 1048576 | tf_op jit(solution)/shard_map/all_to_all | solution.py:287
  84.5 88.4 %copy-start.30 = (f32[1,2048]{1,0:T(1,128)}, f32[1,2048]{1,0:T(1,128)S(1)}, u32[]{:S(2)}) copy-start(f32[1,2048]{1,0:T(1,128)S(1)} %get-tuple-element.351) | copy-start | bytes 24580
  84.6 88.4 %copy-start.32 = (f32[1,2048]{1,0:T(1,128)}, f32[1,2048]{1,0:T(1,128)S(1)}, u32[]{:S(2)}) copy-start(f32[1,2048]{1,0:T(1,128)S(1)} %get-tuple-element.352) | copy-start | bytes 24580
  84.6 88.4 %copy-start.34 = (f32[1,2048]{1,0:T(1,128)}, f32[1,2048]{1,0:T(1,128)S(1)}, u32[]{:S(2)}) copy-start(f32[1,2048]{1,0:T(1,128)S(1)} %get-tuple-element.353) | copy-start | bytes 24580
  84.6 88.4 %copy-start.36 = (f32[1,2048]{1,0:T(1,128)}, f32[1,2048]{1,0:T(1,128)S(1)}, u32[]{:S(2)}) copy-start(f32[1,2048]{1,0:T(1,128)S(1)} %get-tuple-element.354) | copy-start | bytes 24580
  84.6 88.4 %copy-start.38 = (f32[1,2048]{1,0:T(1,128)}, f32[1,2048]{1,0:T(1,128)S(1)}, u32[]{:S(2)}) copy-start(f32[1,2048]{1,0:T(1,128)S(1)} %get-tuple-element.355) | copy-start | bytes 24580
  84.6 88.4 %copy-start.40 = (f32[1,2048]{1,0:T(1,128)}, f32[1,2048]{1,0:T(1,128)S(1)}, u32[]{:S(2)}) copy-start(f32[1,2048]{1,0:T(1,128)S(1)} %get-tuple-element.356) | copy-start | bytes 24580
  84.6 88.4 %copy-start.42 = (f32[1,2048]{1,0:T(1,128)}, f32[1,2048]{1,0:T(1,128)S(1)}, u32[]{:S(2)}) copy-start(f32[1,2048]{1,0:T(1,128)S(1)} %get-tuple-element.357) | copy-start | bytes 24580
  84.6 88.4 %copy-start.44 = (f32[1,2048]{1,0:T(1,128)}, f32[1,2048]{1,0:T(1,128)S(1)}, u32[]{:S(2)}) copy-start(f32[1,2048]{1,0:T(1,128)S(1)} %get-tuple-element.358) | copy-start | bytes 24580
  84.6 88.4 %copy-start.46 = (f32[1,2048]{1,0:T(1,128)}, f32[1,2048]{1,0:T(1,128)S(1)}, u32[]{:S(2)}) copy-start(f32[1,2048]{1,0:T(1,128)S(1)} %get-tuple-element.359) | copy-start | bytes 24580
  84.6 88.4 %copy-start.48 = (f32[1,2048]{1,0:T(1,128)}, f32[1,2048]{1,0:T(1,128)S(1)}, u32[]{:S(2)}) copy-start(f32[1,2048]{1,0:T(1,128)S(1)} %get-tuple-element.360) | copy-start | bytes 24580
  84.6 88.4 %copy-start.50 = (f32[1,2048]{1,0:T(1,128)}, f32[1,2048]{1,0:T(1,128)S(1)}, u32[]{:S(2)}) copy-start(f32[1,2048]{1,0:T(1,128)S(1)} %get-tuple-element.361) | copy-start | bytes 24580
  84.7 88.4 %copy-start.52 = (f32[1,2048]{1,0:T(1,128)}, f32[1,2048]{1,0:T(1,128)S(1)}, u32[]{:S(2)}) copy-start(f32[1,2048]{1,0:T(1,128)S(1)} %get-tuple-element.362) | copy-start | bytes 24580
  84.7 88.4 %copy-start.54 = (f32[1,2048]{1,0:T(1,128)}, f32[1,2048]{1,0:T(1,128)S(1)}, u32[]{:S(2)}) copy-start(f32[1,2048]{1,0:T(1,128)S(1)} %get-tuple-element.363) | copy-start | bytes 24580
  84.7 88.4 %copy-start.56 = (f32[1,2048]{1,0:T(1,128)}, f32[1,2048]{1,0:T(1,128)S(1)}, u32[]{:S(2)}) copy-start(f32[1,2048]{1,0:T(1,128)S(1)} %get-tuple-element.364) | copy-start | bytes 24580
  84.7 88.4 %copy-start.58 = (f32[1,2048]{1,0:T(1,128)}, f32[1,2048]{1,0:T(1,128)S(1)}, u32[]{:S(2)}) copy-start(f32[1,2048]{1,0:T(1,128)S(1)} %get-tuple-element.365) | copy-start | bytes 24580
  84.7 88.4 %copy-start.60 = (f32[1,2048]{1,0:T(1,128)}, f32[1,2048]{1,0:T(1,128)S(1)}, u32[]{:S(2)}) copy-start(f32[1,2048]{1,0:T(1,128)S(1)} %get-tuple-element.366) | copy-start | bytes 24580
  101.9 54.9 %all-to-all-start.2 = ((bf16[128,16,128]{0,2,1:T(8,128)(2,1)}), bf16[128,16,128]{0,2,1:T(8,128)(2,1)S(1)}, u32[]{:S(2)}, u32[]{:S(2)}) async-start(bf16[128,16,128]{0,2,1:T(8,128)(2,1)} %bitcast.24), calls=%async_computation.2 | async-start | bytes 1048576 | tf_op jit(solution)/shard_map/all_to_all | solution.py:289
  156.8 31.2 %all-to-all-start.3 = ((bf16[128,16,128]{2,0,1:T(8,128)(2,1)}), bf16[128,16,128]{2,0,1:T(8,128)(2,1)S(1)}, u32[]{:S(2)}, u32[]{:S(2)}) async-start(bf16[128,16,128]{2,0,1:T(8,128)(2,1)} %copy.195), calls=%async_computation.3 | async-start | bytes 1048576 | tf_op jit(solution)/shard_map/all_to_all | solution.py:288
  258.7 35.5 %all-to-all-start.4 = ((bf16[16,128,128]{1,2,0:T(8,128)(2,1)}), bf16[16,128,128]{1,2,0:T(8,128)(2,1)S(1)}, u32[]{:S(2)}, u32[]{:S(2)}) async-start(bf16[16,128,128]{1,2,0:T(8,128)(2,1)} %copy.198), calls=%async_computation.4 | async-start | bytes 1048576 | tf_op jit(solution)/shard_map/all_to_all | solution.py:295
  275.2 100.6 %copy-start.105 = (pred[128]{0:T(512)(128)(4,1)S(1)}, pred[128]{0:T(512)(128)(4,1)}, u32[]{:S(2)}) copy-start(pred[128]{0:T(512)(128)(4,1)} %get-tuple-element.523) | copy-start | bytes 388
  275.2 100.6 %copy-start.108 = (pred[128]{0:T(512)(128)(4,1)S(1)}, pred[128]{0:T(512)(128)(4,1)}, u32[]{:S(2)}) copy-start(pred[128]{0:T(512)(128)(4,1)} %get-tuple-element.461) | copy-start | bytes 388
  275.2 100.6 %copy-start.109 = (pred[128]{0:T(512)(128)(4,1)S(1)}, pred[128]{0:T(512)(128)(4,1)}, u32[]{:S(2)}) copy-start(pred[128]{0:T(512)(128)(4,1)} %get-tuple-element.470) | copy-start | bytes 388
  275.2 100.6 %copy-start.110 = (pred[128]{0:T(512)(128)(4,1)S(1)}, pred[128]{0:T(512)(128)(4,1)}, u32[]{:S(2)}) copy-start(pred[128]{0:T(512)(128)(4,1)} %get-tuple-element.479) | copy-start | bytes 388
  275.2 100.6 %copy-start.111 = (pred[128]{0:T(512)(128)(4,1)S(1)}, pred[128]{0:T(512)(128)(4,1)}, u32[]{:S(2)}) copy-start(pred[128]{0:T(512)(128)(4,1)} %get-tuple-element.488) | copy-start | bytes 388
  275.2 100.6 %copy-start.121 = (pred[128]{0:T(512)(128)(4,1)S(1)}, pred[128]{0:T(512)(128)(4,1)}, u32[]{:S(2)}) copy-start(pred[128]{0:T(512)(128)(4,1)} %get-tuple-element.497) | copy-start | bytes 388
  294.2 44.5 %all-to-all-start.5 = ((bf16[16,128,128]{2,1,0:T(8,128)(2,1)}), bf16[16,128,128]{2,1,0:T(8,128)(2,1)S(1)}, u32[]{:S(2)}, u32[]{:S(2)}) async-start(bf16[16,128,128]{2,1,0:T(8,128)(2,1)} %copy.199), calls=%async_computation.5 | async-start | bytes 1048576 | tf_op jit(solution)/shard_map/all_to_all | solution.py:296
  338.7 35.3 %all-to-all-start.6 = ((bf16[16,128,128]{2,1,0:T(8,128)(2,1)}), bf16[16,128,128]{2,1,0:T(8,128)(2,1)S(1)}, u32[]{:S(2)}, u32[]{:S(2)}) async-start(bf16[16,128,128]{2,1,0:T(8,128)(2,1)} %copy.201), calls=%async_computation.6 | async-start | bytes 1048576 | tf_op jit(solution)/shard_map/all_to_all | solution.py:297
  374.4 90.9 %collective-permute-start.1 = (bf16[63,2048]{0,1:T(8,128)(2,1)S(1)}, bf16[63,2048]{0,1:T(8,128)(2,1)S(1)}, u32[]{:S(2)}, u32[]{:S(2)}) collective-permute-start(bf16[63,2048]{0,1:T(8,128)(2,1)S(1)} %bitcast.390), channel_id=1, source_target_pairs={{1,0},{2,1},{3,2},{4,3},{5,4},{6,5},{7,6},{8,7},{9,8},{10,9},{11,1... | collective-permute-start | bytes 774152 | tf_op jit(solution)/shard_map/ppermute | solution.py:17
  (104 other events, 5189.3 us)

commit v2 on v1

v2 whole, which is shorter than its diff:
```python
import jax
import jax.numpy as jnp
from jax import lax
from jax.experimental import pallas as pl
from jax.experimental.pallas import tpu as pltpu
from jax.sharding import PartitionSpec as P

HD = 64
REACH = 4
LANES = 128
RIM = 64
GROUP = 2
MESH = pl.DeviceIdType.MESH


def spread_sum(local, scale):
    n_dp, n_seq = lax.axis_size("dp"), lax.axis_size("seq")
    taps, width = local.shape
    lanes = 128
    parts = width // lanes
    split = n_dp // parts
    rows = taps // split

    def kernel(x_ref, o_ref, mine, got, part, gotz, tot, done, s1, r1, s2, r2, s3, r3):
        me = lax.axis_index("dp")
        z = lax.axis_index("seq")
        barrier = pltpu.get_barrier_semaphore()

        def greet_dp(i, _):
            pl.semaphore_signal(barrier, inc=1, device_id={"dp": lax.rem(me + i, n_dp)}, device_id_type=MESH)
            return 0

        def greet_z(i, _):
            pl.semaphore_signal(barrier, inc=1, device_id={"seq": lax.rem(z + i, n_seq)}, device_id_type=MESH)
            return 0

        lax.fori_loop(1, n_dp, greet_dp, 0)
        lax.fori_loop(1, n_seq, greet_z, 0)
        for j in range(n_dp):
            col, row = (j // split) * lanes, (j % split) * rows
            mine[j] = x_ref[row : row + rows, col : col + lanes].astype(jnp.bfloat16)
        pl.semaphore_wait(barrier, n_dp + n_seq - 2)

        def out1(i):
            to = lax.rem(me + i, n_dp)
            return pltpu.make_async_remote_copy(
                src_ref=mine.at[to], dst_ref=got.at[me], send_sem=s1.at[i], recv_sem=r1.at[me],
                device_id={"dp": to}, device_id_type=MESH)

        def in1(i):
            src = lax.rem(me + i, n_dp)
            return pltpu.make_async_remote_copy(
                src_ref=mine.at[src], dst_ref=got.at[src], send_sem=s1.at[i], recv_sem=r1.at[src],
                device_id={"dp": src}, device_id_type=MESH)

        def out2(i):
            to = lax.rem(z + i, n_seq)
            return pltpu.make_async_remote_copy(
                src_ref=part, dst_ref=gotz.at[z], send_sem=s2.at[i], recv_sem=r2.at[z],
                device_id={"seq": to}, device_id_type=MESH)

        def in2(i):
            src = lax.rem(z + i, n_seq)
            return pltpu.make_async_remote_copy(
                src_ref=part, dst_ref=gotz.at[src], send_sem=s2.at[i], recv_sem=r2.at[src],
                device_id={"seq": src}, device_id_type=MESH)

        def out3(i):
            to = lax.rem(me + i, n_dp)
            return pltpu.make_async_remote_copy(
                src_ref=tot, dst_ref=done.at[me], send_sem=s3.at[i], recv_sem=r3.at[me],
                device_id={"dp": to}, device_id_type=MESH)

        def in3(i):
            src = lax.rem(me + i, n_dp)
            return pltpu.make_async_remote_copy(
                src_ref=tot, dst_ref=done.at[src], send_sem=s3.at[i], recv_sem=r3.at[src],
                device_id={"dp": src}, device_id_type=MESH)

        def start(make, count):
            def body(i, _):
                make(i).start()
                return 0
            lax.fori_loop(1, count, body, 0)

        def sent(make, count):
            def body(i, _):
                make(i).wait_send()
                return 0
            lax.fori_loop(1, count, body, 0)

        def landed(make, count):
            def body(i, _):
                make(i).wait_recv()
                return 0
            lax.fori_loop(1, count, body, 0)

        start(out1, n_dp)
        got[me] = mine[me]
        landed(in1, n_dp)
        total = got[0].astype(jnp.float32)
        for j in range(1, n_dp):
            total = total + got[j].astype(jnp.float32)
        part[...] = total.astype(jnp.bfloat16)
        start(out2, n_seq)
        gotz[z] = part[...]
        landed(in2, n_seq)
        total = gotz[0].astype(jnp.float32)
        for j in range(1, n_seq):
            total = total + gotz[j].astype(jnp.float32)
        tot[...] = (total * scale).astype(jnp.bfloat16)
        start(out3, n_dp)
        done[me] = tot[...]
        landed(in3, n_dp)
        for j in range(n_dp):
            col, row = (j // split) * lanes, (j % split) * rows
            o_ref[row : row + rows, col : col + lanes] = done[j].astype(jnp.float32)
        sent(out1, n_dp)
        sent(out2, n_seq)
        sent(out3, n_dp)

    piece = (rows, lanes)
    return pl.pallas_call(
        kernel,
        out_shape=jax.ShapeDtypeStruct((taps, width), jnp.float32),
        in_specs=[pl.BlockSpec(memory_space=pltpu.VMEM)],
        out_specs=pl.BlockSpec(memory_space=pltpu.VMEM),
        scratch_shapes=[
            pltpu.VMEM((n_dp,) + piece, jnp.bfloat16),
            pltpu.VMEM((n_dp,) + piece, jnp.bfloat16),
            pltpu.VMEM(piece, jnp.bfloat16),
            pltpu.VMEM((n_seq,) + piece, jnp.bfloat16),
            pltpu.VMEM(piece, jnp.bfloat16),
            pltpu.VMEM((n_dp,) + piece, jnp.bfloat16),
            pltpu.SemaphoreType.DMA((n_dp,)),
            pltpu.SemaphoreType.DMA((n_dp,)),
            pltpu.SemaphoreType.DMA((n_seq,)),
            pltpu.SemaphoreType.DMA((n_seq,)),
            pltpu.SemaphoreType.DMA((n_dp,)),
            pltpu.SemaphoreType.DMA((n_dp,)),
        ],
        compiler_params=pltpu.CompilerParams(collective_id=1, has_side_effects=True),
        name="spread_sum",
    )(local)


def timeline(query, key_rows, feats, grad, ids, picked, weight):
    n_seq = lax.axis_size("seq")
    rows, width = query.shape
    taps = weight.shape[0]
    tiles = width // LANES
    chunks = tiles // GROUP
    scale = HD ** (-0.5)
    span = (REACH + 1) * rows
    shifted_rows = rows + RIM - 8
    f32, bf16 = jnp.float32, jnp.bfloat16

    def kernel(
        q_ref, k_ref, e_ref, g_ref, id_ref, pick_ref, w_ref,
        dq_ref, dk_ref, de_ref, f_ref,
        win, part, out_buf, in_buf, e_halo, v_halo, vg, e_src,
        id_src, id_buf, cap, left, right, ext, moved,
        win_s, win_r, back_s, back_r, eh_s, eh_r, vh_s, vh_r, id_s, id_r,
    ):
        me = lax.axis_index("seq")

        def at(offset):
            return lax.rem(me + offset + n_seq, n_seq)

        up, down = at(1), at(-1)

        def remote(src, dst, send, recv, to):
            return pltpu.make_async_remote_copy(
                src_ref=src, dst_ref=dst, send_sem=send, recv_sem=recv,
                device_id={"seq": to}, device_id_type=MESH,
            )

        def cols(tile):
            return pl.ds(pl.multiple_of(tile * LANES, LANES), LANES)

        def group(c):
            return pl.ds(c * GROUP, GROUP)

        def fwd(c, d):
            return remote(
                win.at[:, group(c), pl.ds((d - 1) * rows, rows), :],
                win.at[:, group(c), pl.ds(d * rows, rows), :],
                win_s.at[c, d - 1], win_r.at[c, d - 1], up,
            )

        def back(c, d):
            return remote(
                out_buf.at[:, group(c), pl.ds((d - 1) * rows, rows), :],
                in_buf.at[:, group(c), pl.ds((d - 1) * rows, rows), :],
                back_s.at[c, d - 1], back_r.at[c, d - 1], down,
            )

        def events_halo(c):
            return remote(
                e_src.at[group(c)], e_halo.at[group(c)], eh_s.at[c], eh_r.at[c], up
            )

        def grads_halo(c):
            return remote(
                vg.at[group(c), pl.ds(0, RIM), :], v_halo.at[group(c)], vh_s.at[c], vh_r.at[c], down
            )

        def ids_to(slot):
            to = down if slot == 0 else at(slot)
            return remote(id_src, id_buf.at[slot], id_s.at[slot], id_r.at[slot], to)

        barrier = pltpu.get_barrier_semaphore()
        for offset in range(1, REACH + 1):
            for to in (at(offset), at(-offset)):
                pl.semaphore_signal(barrier, inc=1, device_id={"seq": to}, device_id_type=MESH)
        own_ids = id_ref[...].astype(f32)
        id_src[...] = jnp.broadcast_to(own_ids, id_src.shape)

        def stage(tile, _):
            win[0, tile, pl.ds(0, rows), :] = k_ref[:, cols(tile)]
            e_src[tile] = e_ref[pl.ds(rows - RIM, RIM), cols(tile)]
            return 0

        lax.fori_loop(0, tiles, stage, 0)
        pl.semaphore_wait(barrier, 2 * REACH)
        for slot in range(REACH + 1):
            ids_to(slot).start()

        def start_halo(c, _):
            events_halo(c).start()
            return 0

        lax.fori_loop(0, chunks, start_halo, 0)
        for slot in range(REACH + 1):
            ids_to(slot).wait_recv()

        square = (rows, rows)
        own_row = jnp.broadcast_to(own_ids, square)

        def same(row):
            col = jnp.broadcast_to(row, square).T
            return jnp.where(col == own_row, 1.0, 0.0)

        s_at = lax.broadcasted_iota(jnp.int32, square, 0)
        r_at = lax.broadcasted_iota(jnp.int32, square, 1)
        here = same(own_ids)
        low = jnp.where(s_at <= r_at, here, 0.0)
        high = jnp.where(s_at >= r_at, here, 0.0)
        before = same(id_buf[1][0:1]) * jnp.where(me > 0, 1.0, 0.0)
        after = same(id_buf[0][0:1]) * jnp.where(me < n_seq - 1, 1.0, 0.0)
        reach_left = jnp.sum(low, axis=0, keepdims=True) + jnp.sum(before, axis=0, keepdims=True) - 1.0
        reach_right = jnp.sum(high, axis=0, keepdims=True) + jnp.sum(after, axis=0, keepdims=True) - 1.0
        left[...] = jnp.broadcast_to(reach_left, square).T
        right[...] = jnp.broadcast_to(reach_right, square).T
        for d in range(REACH + 1):
            open_pairs = low if d == 0 else same(id_buf[d][0:1])
            open_pairs = open_pairs * jnp.broadcast_to(pick_ref[d : d + 1, :], square)
            limit = jnp.where(open_pairs > 0.5, 3.0e38, -1.0e30)
            cap[d * rows : (d + 1) * rows, 0:rows] = limit
            cap[d * rows : (d + 1) * rows, rows : 2 * rows] = limit

        def shift_back():
            for k in range(8):
                moved[k] = ext[8 - k : 8 - k + shifted_rows, :]

        def load_events(tile):
            ext[0:RIM, :] = e_halo[tile].astype(f32)
            ext[RIM : RIM + rows, :] = e_ref[:, cols(tile)].astype(f32)
            shift_back()

        def taps_at(q, tile):
            return w_ref[pl.ds(pl.multiple_of(q * 8, 8), 8), cols(tile)]

        def conv(tile):
            load_events(tile)
            reach = left[...]

            def body(q, total):
                tap_rows = taps_at(q, tile)
                base = pl.multiple_of(RIM - 8 - 8 * q, 8)
                first = (q * 8).astype(f32)
                for k in range(8):
                    piece = moved[k, pl.ds(base, rows), :]
                    total = total + jnp.where(reach >= first + k, piece * tap_rows[k : k + 1, :], 0.0)
                return total

            total = lax.fori_loop(0, taps // 8, body, jnp.zeros((rows, LANES), f32))
            win[1, tile, pl.ds(0, rows), :] = total.astype(bf16)

        def conv_chunk(c):
            events_halo(c).wait_recv()
            for j in range(GROUP):
                conv(c * GROUP + j)

        def attend(tile):
            lane = lax.broadcasted_iota(jnp.int32, (rows, LANES), 1)
            first = lane < HD

            def pair(ref):
                both = ref[:, cols(tile)].astype(f32)
                return jnp.concatenate(
                    [jnp.where(first, both, 0.0), jnp.where(first, 0.0, both)], axis=0
                ).astype(bf16)

            q2, g2 = pair(q_ref), pair(g_ref)
            keys, vals = win[0, tile], win[1, tile]
            last = (((1,), (1,)), ((), ()))
            scores = lax.dot_general(keys, q2, last, preferred_element_type=f32)
            scores = jnp.minimum(scores * scale, cap[...])
            top = jnp.max(scores, axis=0, keepdims=True)
            raw = jnp.exp(scores - top)
            probs = raw * (1.0 / jnp.sum(raw, axis=0, keepdims=True))
            low_probs = probs.astype(bf16)
            dprobs = lax.dot_general(vals, g2, last, preferred_element_type=f32)
            delta = jnp.sum(low_probs.astype(f32) * dprobs, axis=0, keepdims=True)
            dscores = (probs * (dprobs - delta)).astype(bf16)
            dq2 = lax.dot_general(
                dscores, keys, (((0,), (0,)), ((), ())), preferred_element_type=f32
            )
            dq = jnp.where(first, dq2[0:rows], dq2[rows : 2 * rows]) * scale
            dq_ref[:, cols(tile)] = dq.astype(bf16)
            mid = (((1,), (0,)), ((), ()))
            part[0, tile] = lax.dot_general(dscores, q2, mid, preferred_element_type=f32) * scale
            part[1, tile] = lax.dot_general(low_probs, g2, mid, preferred_element_type=f32)

        def give(c, d):
            at_d = pl.ds(d * rows, rows)
            total = part[:, group(c), at_d, :]
            if d < REACH:
                back(c, d + 1).wait_recv()
                total = total + in_buf[:, group(c), at_d, :].astype(f32)
            out_buf[:, group(c), pl.ds((d - 1) * rows, rows), :] = total.astype(bf16)
            back(c, d).start()

        def settle(c):
            back(c, 1).wait_recv()
            for j in range(GROUP):
                tile = c * GROUP + j
                total = part[:, tile, pl.ds(0, rows), :] + in_buf[:, tile, pl.ds(0, rows), :].astype(f32)
                low_total = total.astype(bf16)
                dk_ref[:, cols(tile)] = low_total[0]
                vg[tile] = low_total[1]
            grads_halo(c).start()

        def finish(tile):
            own = vg[tile].astype(f32)
            ext[0:rows, :] = own
            ext[rows : rows + RIM, :] = v_halo[tile].astype(f32)
            for k in range(8):
                moved[k] = ext[k : k + shifted_rows, :]
            reach = right[...]

            def body(q, total):
                tap_rows = taps_at(q, tile)
                base = pl.multiple_of(8 * q, 8)
                first = (q * 8).astype(f32)
                for k in range(8):
                    piece = moved[k, pl.ds(base, rows), :]
                    total = total + jnp.where(reach >= first + k, piece * tap_rows[k : k + 1, :], 0.0)
                return total

            total = lax.fori_loop(0, taps // 8, body, jnp.zeros((rows, LANES), f32))
            de_ref[:, cols(tile)] = total.astype(bf16)
            load_events(tile)
            reach_l = left[...]

            def tap_body(q, _):
                base = pl.multiple_of(RIM - 8 - 8 * q, 8)
                first = (q * 8).astype(f32)
                sums = []
                for k in range(8):
                    piece = moved[k, pl.ds(base, rows), :]
                    kept = jnp.where(reach_l >= first + k, piece * own, 0.0)
                    sums.append(jnp.sum(kept, axis=0, keepdims=True))
                f_ref[pl.ds(pl.multiple_of(q * 8, 8), 8), cols(tile)] = jnp.concatenate(sums, axis=0)
                return 0

            lax.fori_loop(0, taps // 8, tap_body, 0)

        def finish_chunk(c):
            grads_halo(c).wait_recv()
            for j in range(GROUP):
                finish(c * GROUP + j)

        def early(c, _):
            conv_chunk(c)
            return 0

        lax.fori_loop(0, min(2, chunks), early, 0)
        fwd(0, 1).start()

        def tick(i, _):
            a, b, z = i - 1, i - 2, i - 3
            on_f = i < chunks
            on_a = jnp.logical_and(a >= 0, a < chunks)
            on_b = jnp.logical_and(b >= 0, b < chunks)
            on_z = jnp.logical_and(z >= 0, z < chunks)

            @pl.when(i + 1 < chunks)
            def _():
                fwd(i + 1, 1).start()

            @pl.when(on_z)
            def _():
                settle(z)

            for s in range(REACH):
                @pl.when(on_b)
                def _():
                    give(b, REACH - s)

                @pl.when(on_f)
                def _():
                    fwd(i, s + 1).wait_recv()
                    if s + 1 < REACH:
                        fwd(i, s + 2).start()

                if s < GROUP:
                    @pl.when(on_a)
                    def _():
                        attend(a * GROUP + s)

                if s == 2:
                    @pl.when(i + 2 < chunks)
                    def _():
                        conv_chunk(i + 2)

                if s == 3:
                    @pl.when(on_z)
                    def _():
                        finish_chunk(z)

            return 0

        lax.fori_loop(0, chunks + 3, tick, 0)

        for slot in range(REACH + 1):
            ids_to(slot).wait_send()

        def drain(c, _):
            events_halo(c).wait_send()
            grads_halo(c).wait_send()
            for d in range(1, REACH + 1):
                fwd(c, d).wait_send()
                back(c, d).wait_send()
            return 0

        lax.fori_loop(0, chunks, drain, 0)

    vmem = pl.BlockSpec(memory_space=pltpu.VMEM)
    sems = pltpu.SemaphoreType.DMA
    tall = jax.ShapeDtypeStruct((rows, width), bf16)
    return pl.pallas_call(
        kernel,
        out_shape=(tall, tall, tall, jax.ShapeDtypeStruct((taps, width), f32)),
        in_specs=[vmem] * 7,
        out_specs=(vmem,) * 4,
        scratch_shapes=[
            pltpu.VMEM((2, tiles, span, LANES), bf16),
            pltpu.VMEM((2, tiles, span, LANES), f32),
            pltpu.VMEM((2, tiles, span - rows, LANES), bf16),
            pltpu.VMEM((2, tiles, span - rows, LANES), bf16),
            pltpu.VMEM((tiles, RIM, LANES), bf16),
            pltpu.VMEM((tiles, RIM, LANES), bf16),
            pltpu.VMEM((tiles, rows, LANES), bf16),
            pltpu.VMEM((tiles, RIM, LANES), bf16),
            pltpu.VMEM((8, LANES), f32),
            pltpu.VMEM((REACH + 1, 8, LANES), f32),
            pltpu.VMEM((span, 2 * rows), f32),
            pltpu.VMEM((rows, LANES), f32),
            pltpu.VMEM((rows, LANES), f32),
            pltpu.VMEM((rows + RIM, LANES), f32),
            pltpu.VMEM((8, shifted_rows, LANES), f32),
            sems((chunks, REACH)), sems((chunks, REACH)),
            sems((chunks, REACH)), sems((chunks, REACH)),
            sems((chunks,)), sems((chunks,)), sems((chunks,)), sems((chunks,)),
            sems((REACH + 1,)), sems((REACH + 1,)),
        ],
        compiler_params=pltpu.CompilerParams(
            collective_id=0, has_side_effects=True, vmem_limit_bytes=48 * 1024 * 1024
        ),
        name="timeline",
    )(query, key_rows, feats, grad, ids, picked, weight)


def per_device(queries, keys, events, out_grad, segment_ids, block_list, conv_weight):
    blist = block_list[0]
    shards = lax.axis_size("dp") * lax.axis_size("seq")
    here = lax.axis_index("seq")
    own = lax.dynamic_slice_in_dim(blist, here, 1, 0)
    wanted = here - jnp.arange(8, dtype=jnp.int32)
    hit = jnp.any(own == wanted[:, None], axis=1) & (wanted >= 0)
    picked = jnp.broadcast_to(hit.astype(jnp.float32)[:, None], (8, LANES))
    q_grad, k_grad, e_grad, f_local = timeline(
        queries[0], keys[0], events[0], out_grad[0], segment_ids, picked, conv_weight
    )
    f_grad = spread_sum(f_local, 1.0 / shards)
    return (q_grad[None], k_grad[None], e_grad[None], f_grad)


def solution(mesh):
    in_specs = (
        P("dp", "seq", None),
        P("dp", "seq", None),
        P("dp", "seq", None),
        P("dp", "seq", None),
        P("dp", "seq"),
        P("dp", None, None),
        P(),
    )
    out_specs = (P("dp", "seq", None), P("dp", "seq", None), P("dp", "seq", None), P())
    return jax.shard_map(
        per_device, mesh=mesh, in_specs=in_specs, out_specs=out_specs, check_vma=False
    )
```

time: 520 us -> 270 us (0.52); the launches traced: 510 us -> 269 us
  Pallas kernels: 41.7 us -> 257 us
  other arithmetic: 141 us -> 0.1 us
  starting transfers between devices: 103 us -> 0 us
  waiting for transfers between devices: 84.9 us -> 0 us
  blocking collectives: 46.4 us -> 0 us
  local copies, waits for them, and re-layouts: 53.6 us -> 11.1 us
  matrix products: 35.5 us -> 0 us
    pallas_call x0 -> x1, Pallas kernels: none -> 192 us  [timeline(): pl.pallas_call(kernel, out_shape=(tall, tall, tall, jax.ShapeDtypeStruct(...]
    all_to_all x7 -> x0, starting transfers between devices: 98.4 us -> none  [the longest x1 22.1 us: per_device(): lax.all_to_all(k_grad, 'seq', split_axis=0, concat_axis=1, tiled=True)]
    all_to_all x7 -> x0, waiting for transfers between devices: 84.9 us -> none  [the longest x1 21 us: per_device(): lax.all_to_all(k_grad, 'seq', split_axis=0, concat_axis=1, tiled=True)]
    reduce_sum x15 -> x0, other arithmetic: 47.5 us -> none  [the longest x11 41.1 us: tap_gradient(): sums.append(jnp.sum(jnp.where(match, piece * grad_wide, 0.0), axis=0))]
    all_gather x1 -> x0, blocking collectives: 46.4 us -> none  [per_device(): all_ids = lax.all_gather(segment_ids, 'seq', axis=1, tiled=True)[0]]
    broadcast_in_dim x1 -> x0, other arithmetic: 41.2 us -> none  [per_device(): return (q_back[None], k_back[None], e_grad[None], f_grad)]
    convert_element_type x1, other arithmetic: 40.2 us -> 0.01 us  [per_device(): picked = jnp.broadcast_to(hit.astype(jnp.float32)[:, None], (8, LANES))]
    dot_general x20 -> x0, matrix products: 35.5 us -> none  [the longest x16 26.3 us: contract(): return jnp.einsum(form, left, right, preferred_element_type=jnp.float32)]
  transfers between devices with their start and end apart: 9 -> 0, of which waited for: 5 -> 0; matrix products, arithmetic and copies ran while one was open for 22% -> 0% of each run, Pallas kernels for 8% -> 0%
where the time goes in v2:
time: 270 us; the launch traced here: 269 us
  Pallas kernels  257 us (95%)
  local copies, waits for them, and re-layouts  11.1 us (4%)
    pallas_call x1, Pallas kernels, timeline(): pl.pallas_call(kernel, out_shape=(tall, tall, tall, jax.ShapeDtypeStruct(...  192 us
    pallas_call x1, Pallas kernels, spread_sum(): pl.pallas_call(kernel, out_shape=jax.ShapeDtypeStruct((taps, width), jnp....  65 us
    unnamed x22, local copies, waits for them, and re-layouts  10.9 us

profile of v2, /device:TPU:1, one launch (start us, length us, event | category | flops | bytes accessed | tf_op | source)
XLA Modules:
  0.0 269.2 jit_solution(7053291090685562792)
XLA Ops:
  0.6 0.0 copy-start
  0.6 0.7 copy-done
  1.3 0.2 dynamic-slice_reduce_fusion
  1.5 0.1 compare_reduce_fusion
  1.6 0.0 copy-start.7
  1.6 0.1 broadcast_in_dim.16.pick_ref
  1.7 0.6 copy-done.7
  2.3 0.0 copy-start.2
  2.3 1.0 copy-done.2
  3.3 0.0 copy-start.3
  3.3 1.0 copy-done.3
  4.3 0.0 copy-start.4
  4.4 1.0 copy-done.4
  5.4 0.0 copy-start.5
  5.4 1.0 copy-done.5
  6.4 0.0 copy-start.6
  6.4 1.0 copy-done.6
  7.5 192.3 %timeline.1 = (bf16[128,2048]{1,0:T(8,128)(2,1)S(1)}, bf16[128,2048]{1,0:T(8,128)(2,1)S(1)}, bf16[128,2048]{1,0:T(8,128)(2,1)S(1)}, f32[64,2048]{1,0:T(8,128)S(1)}) custom-call(bf16[128,2048]{1,0:T(8,128)(2,1)S(1)} %bitcast.10, bf16[128,2048]{1,0:T(8,128)(2,1)S(1)} %bitcast.11, bf16[128,2048]{1,0:T(8,128)(2,1)S(1)} %bitcast.12, ...), custom_call_target="tpu_custom_call" | custom-call | tf_op jit(solution)/shard_map/timeline/pallas_call | solution.py:453
  199.8 0.0 copy-start.1
  199.8 0.8 copy-done.1
  200.6 65.0 %spread_sum.1 = f32[64,2048]{1,0:T(8,128)} custom-call(f32[64,2048]{1,0:T(8,128)} %copy-done.1), custom_call_target="tpu_custom_call" | custom-call | tf_op jit(solution)/shard_map/spread_sum/pallas_call | solution.py:123
  265.6 0.8 copy.15
  266.4 0.8 copy.16
  267.2 0.0 copy-start.8
  267.2 0.8 copy.17
  268.0 0.4 copy-done.8
  268.4 0.8 copy.18
  (2 shorter events, 0.0 us)
Async XLA Ops:
  0.6 0.7 copy-start
  1.6 0.7 copy-start.7
  2.3 1.0 copy-start.2
  3.3 1.0 copy-start.3
  4.3 1.0 copy-start.4
  5.4 1.0 copy-start.5
  6.4 1.0 copy-start.6
  199.8 0.8 copy-start.1
  267.2 1.2 copy-start.8

commit v3 on v2

v3 whole, which is shorter than its diff:
```python
import jax
import jax.numpy as jnp
from jax import lax
from jax.experimental import pallas as pl
from jax.experimental.pallas import tpu as pltpu
from jax.sharding import PartitionSpec as P

HD = 64
REACH = 4
LANES = 128
RIM = 64
BATCH = 4
MESH = pl.DeviceIdType.MESH


def timeline(query, key_rows, feats, grad, ids, picked, weight):
    n_dp, n_seq = lax.axis_size("dp"), lax.axis_size("seq")
    rows, width = query.shape
    taps = weight.shape[0]
    tiles = width // LANES
    batch = min(BATCH, tiles)
    split = n_dp // tiles
    piece = taps // split
    mean = 1.0 / (n_dp * n_seq)
    scale = HD ** (-0.5)
    span = (REACH + 1) * rows
    shifted_rows = rows + RIM - 8
    f32, bf16 = jnp.float32, jnp.bfloat16

    def kernel(
        q_in, k_in, e_in, g_in, id_ref, pick_ref, w_in,
        dq_ref, dk_ref, de_ref, f_out,
        win, part, out_buf, in_buf, e_halo, v_halo, vg, e_src,
        id_src, id_buf, cap, left, right, ext, moved,
        q_ref, k_ref, e_ref, g_ref, w_ref, load_s,
        f_ref, mine, got, part_sum, got_z, total_sum, whole, sum_s, sum_r,
        win_s, win_r, back_s, back_r, eh_s, eh_r, vh_s, vh_r, id_s, id_r,
    ):
        me, lane_me = lax.axis_index("seq"), lax.axis_index("dp")

        def at(offset):
            return lax.rem(me + offset + n_seq, n_seq)

        up, down = at(1), at(-1)

        def remote(src, dst, send, recv, to):
            return pltpu.make_async_remote_copy(
                src_ref=src, dst_ref=dst, send_sem=send, recv_sem=recv,
                device_id={"seq": to}, device_id_type=MESH,
            )

        def cols(tile):
            return pl.ds(pl.multiple_of(tile * LANES, LANES), LANES)

        def fwd(t, d):
            return remote(
                win.at[:, t, pl.ds((d - 1) * rows, rows), :],
                win.at[:, t, pl.ds(d * rows, rows), :],
                win_s.at[t, d - 1], win_r.at[t, d - 1], up,
            )

        def back(t, d):
            return remote(
                out_buf.at[:, t, pl.ds((d - 1) * rows, rows), :],
                in_buf.at[:, t, pl.ds((d - 1) * rows, rows), :],
                back_s.at[t, d - 1], back_r.at[t, d - 1], down,
            )

        def events_halo(n):
            several = pl.ds(n * batch, batch)
            return remote(e_src.at[several], e_halo.at[several], eh_s.at[n], eh_r.at[n], up)

        def grads_halo(t):
            return remote(
                vg.at[t, pl.ds(0, RIM), :], v_halo.at[t], vh_s.at[t], vh_r.at[t], down
            )

        def ids_to(slot):
            to = down if slot == 0 else at(slot)
            return remote(id_src, id_buf.at[slot], id_s.at[slot], id_r.at[slot], to)

        loads = [
            pltpu.make_async_copy(src, dst, load_s.at[n])
            for n, (src, dst) in enumerate(
                ((e_in, e_ref), (k_in, k_ref), (w_in, w_ref), (q_in, q_ref), (g_in, g_ref))
            )
        ]
        for load in loads:
            load.start()
        barrier = pltpu.get_barrier_semaphore()

        def greet_seq(n, _):
            pl.semaphore_signal(barrier, inc=1, device_id={"seq": at(n)}, device_id_type=MESH)
            return 0

        def greet_dp(n, _):
            to = lax.rem(lane_me + n, n_dp)
            pl.semaphore_signal(barrier, inc=1, device_id={"dp": to}, device_id_type=MESH)
            return 0

        lax.fori_loop(1, n_seq, greet_seq, 0)
        lax.fori_loop(1, n_dp, greet_dp, 0)
        own_ids = id_ref[...].astype(f32)
        id_src[...] = jnp.broadcast_to(own_ids, id_src.shape)

        for load in loads:
            load.wait()

        def stage(tile, _):
            win[0, tile, pl.ds(0, rows), :] = k_ref[:, cols(tile)]
            e_src[tile] = e_ref[pl.ds(rows - RIM, RIM), cols(tile)]
            return 0

        lax.fori_loop(0, tiles, stage, 0)
        pl.semaphore_wait(barrier, n_seq + n_dp - 2)
        for slot in range(REACH + 1):
            ids_to(slot).start()

        def start_halo(c, _):
            events_halo(c).start()
            return 0

        lax.fori_loop(0, tiles // batch, start_halo, 0)
        for slot in range(REACH + 1):
            ids_to(slot).wait_recv()

        square = (rows, rows)
        own_row = jnp.broadcast_to(own_ids, square)

        def same(row):
            col = jnp.broadcast_to(row, square).T
            return jnp.where(col == own_row, 1.0, 0.0)

        s_at = lax.broadcasted_iota(jnp.int32, square, 0)
        r_at = lax.broadcasted_iota(jnp.int32, square, 1)
        here = same(own_ids)
        low = jnp.where(s_at <= r_at, here, 0.0)
        high = jnp.where(s_at >= r_at, here, 0.0)
        before = same(id_buf[1][0:1]) * jnp.where(me > 0, 1.0, 0.0)
        after = same(id_buf[0][0:1]) * jnp.where(me < n_seq - 1, 1.0, 0.0)
        reach_left = jnp.sum(low, axis=0, keepdims=True) + jnp.sum(before, axis=0, keepdims=True) - 1.0
        reach_right = jnp.sum(high, axis=0, keepdims=True) + jnp.sum(after, axis=0, keepdims=True) - 1.0
        left[...] = jnp.broadcast_to(reach_left, square).T
        right[...] = jnp.broadcast_to(reach_right, square).T
        for d in range(REACH + 1):
            open_pairs = low if d == 0 else same(id_buf[d][0:1])
            open_pairs = open_pairs * jnp.broadcast_to(pick_ref[d : d + 1, :], square)
            limit = jnp.where(open_pairs > 0.5, 3.0e38, -1.0e30)
            cap[d * rows : (d + 1) * rows, 0:rows] = limit
            cap[d * rows : (d + 1) * rows, rows : 2 * rows] = limit

        def shift_back():
            for k in range(8):
                moved[k] = ext[8 - k : 8 - k + shifted_rows, :]

        def load_events(tile):
            ext[0:RIM, :] = e_halo[tile].astype(f32)
            ext[RIM : RIM + rows, :] = e_ref[:, cols(tile)].astype(f32)
            shift_back()

        def taps_at(q, tile):
            return w_ref[pl.ds(pl.multiple_of(q * 8, 8), 8), cols(tile)]

        def conv(tile):
            load_events(tile)
            reach = left[...]

            def body(q, total):
                tap_rows = taps_at(q, tile)
                base = pl.multiple_of(RIM - 8 - 8 * q, 8)
                first = (q * 8).astype(f32)
                for k in range(8):
                    piece = moved[k, pl.ds(base, rows), :]
                    total = total + jnp.where(reach >= first + k, piece * tap_rows[k : k + 1, :], 0.0)
                return total

            total = lax.fori_loop(0, taps // 8, body, jnp.zeros((rows, LANES), f32))
            win[1, tile, pl.ds(0, rows), :] = total.astype(bf16)

        def conv_next(tile):
            @pl.when(lax.rem(tile, batch) == 0)
            def _():
                events_halo(tile // batch).wait_recv()

            conv(tile)

        def attend(tile):
            lane = lax.broadcasted_iota(jnp.int32, (rows, LANES), 1)
            first = lane < HD

            def pair(ref):
                both = ref[:, cols(tile)].astype(f32)
                return jnp.concatenate(
                    [jnp.where(first, both, 0.0), jnp.where(first, 0.0, both)], axis=0
                ).astype(bf16)

            q2, g2 = pair(q_ref), pair(g_ref)
            keys, vals = win[0, tile], win[1, tile]
            last = (((1,), (1,)), ((), ()))
            scores = lax.dot_general(keys, q2, last, preferred_element_type=f32)
            scores = jnp.minimum(scores * scale, cap[...])
            top = jnp.max(scores, axis=0, keepdims=True)
            raw = jnp.exp(scores - top)
            probs = raw * (1.0 / jnp.sum(raw, axis=0, keepdims=True))
            low_probs = probs.astype(bf16)
            dprobs = lax.dot_general(vals, g2, last, preferred_element_type=f32)
            delta = jnp.sum(low_probs.astype(f32) * dprobs, axis=0, keepdims=True)
            dscores = (probs * (dprobs - delta)).astype(bf16)
            dq2 = lax.dot_general(
                dscores, keys, (((0,), (0,)), ((), ())), preferred_element_type=f32
            )
            dq = jnp.where(first, dq2[0:rows], dq2[rows : 2 * rows]) * scale
            dq_ref[:, cols(tile)] = dq.astype(bf16)
            mid = (((1,), (0,)), ((), ()))
            part[0, tile] = lax.dot_general(dscores, q2, mid, preferred_element_type=f32) * scale
            part[1, tile] = lax.dot_general(low_probs, g2, mid, preferred_element_type=f32)

        def give(t, d):
            at_d = pl.ds(d * rows, rows)
            total = part[:, t, at_d, :]
            if d < REACH:
                back(t, d + 1).wait_recv()
                total = total + in_buf[:, t, at_d, :].astype(f32)
            out_buf[:, t, pl.ds((d - 1) * rows, rows), :] = total.astype(bf16)
            back(t, d).start()

        def settle(t):
            back(t, 1).wait_recv()
            total = part[:, t, pl.ds(0, rows), :] + in_buf[:, t, pl.ds(0, rows), :].astype(f32)
            low_total = total.astype(bf16)
            dk_ref[:, cols(t)] = low_total[0]
            vg[t] = low_total[1]
            grads_halo(t).start()

        def events_back(tile):
            grads_halo(tile).wait_recv()
            own = vg[tile].astype(f32)
            ext[0:rows, :] = own
            ext[rows : rows + RIM, :] = v_halo[tile].astype(f32)
            for k in range(8):
                moved[k] = ext[k : k + shifted_rows, :]
            reach = right[...]

            def body(q, total):
                tap_rows = taps_at(q, tile)
                base = pl.multiple_of(8 * q, 8)
                first = (q * 8).astype(f32)
                for k in range(8):
                    piece = moved[k, pl.ds(base, rows), :]
                    total = total + jnp.where(reach >= first + k, piece * tap_rows[k : k + 1, :], 0.0)
                return total

            total = lax.fori_loop(0, taps // 8, body, jnp.zeros((rows, LANES), f32))
            de_ref[:, cols(tile)] = total.astype(bf16)

        def tap_sums(tile):
            own = vg[tile].astype(f32)
            load_events(tile)
            reach_l = left[...]

            def tap_body(q, _):
                base = pl.multiple_of(RIM - 8 - 8 * q, 8)
                first = (q * 8).astype(f32)
                sums = []
                for k in range(8):
                    piece = moved[k, pl.ds(base, rows), :]
                    kept = jnp.where(reach_l >= first + k, piece * own, 0.0)
                    sums.append(jnp.sum(kept, axis=0, keepdims=True))
                f_ref[pl.ds(pl.multiple_of(q * 8, 8), 8), :] = jnp.concatenate(sums, axis=0)
                return 0

            lax.fori_loop(0, taps // 8, tap_body, 0)
            share(tile)

        def to_dp(src, dst, n, to):
            return pltpu.make_async_remote_copy(
                src_ref=src, dst_ref=dst, send_sem=sum_s.at[n], recv_sem=sum_r.at[n],
                device_id={"dp": to}, device_id_type=MESH,
            )

        def share(tile):
            for h in range(split):
                owner = tile * split + h
                mine[owner] = f_ref[h * piece : (h + 1) * piece, :].astype(bf16)

                @pl.when(owner == lane_me)
                def _():
                    got[owner] = mine[owner]

                @pl.when(owner != lane_me)
                def _():
                    to_dp(mine.at[owner], got.at[lane_me], 0, owner).start()

        def settled(ref, n, count):
            pltpu.make_async_copy(ref.at[pl.ds(0, count)], ref.at[pl.ds(0, count)], n).wait()

        def sum_all():
            settled(got, sum_r.at[0], n_dp - 1)
            total = got[0].astype(f32)
            for n in range(1, n_dp):
                total = total + got[n].astype(f32)
            part_sum[...] = total.astype(bf16)

            def send_z(n, _):
                remote(part_sum, got_z.at[me], sum_s.at[1], sum_r.at[1], at(n)).start()
                return 0

            lax.fori_loop(1, n_seq, send_z, 0)
            got_z[me] = part_sum[...]
            settled(got_z, sum_r.at[1], n_seq - 1)
            total = got_z[0].astype(f32)
            for n in range(1, n_seq):
                total = total + got_z[n].astype(f32)
            total_sum[...] = (total * mean).astype(bf16)

            def send_dp(n, _):
                to_dp(total_sum, whole.at[lane_me], 2, lax.rem(lane_me + n, n_dp)).start()
                return 0

            lax.fori_loop(1, n_dp, send_dp, 0)
            whole[lane_me] = total_sum[...]
            settled(whole, sum_r.at[2], n_dp - 1)
            for n in range(n_dp):
                col, row = (n // split) * LANES, (n % split) * piece
                f_out[row : row + piece, col : col + LANES] = whole[n].astype(f32)
            settled(mine, sum_s.at[0], n_dp - 1)
            settled(got_z, sum_s.at[1], n_seq - 1)
            settled(whole, sum_s.at[2], n_dp - 1)

        conv_next(0)
        conv_next(1)

        def tick(i, _):
            def on(t, act):
                @pl.when(jnp.logical_and(t >= 0, t < tiles))
                def _():
                    act(t)

            def pass_on(t, d):
                fwd(t, d - 1).wait_recv()
                fwd(t, d).start()

            def meet(t):
                fwd(t, REACH).wait_recv()
                attend(t)

            on(i, lambda t: fwd(t, 1).start())
            on(i - 5, lambda t: give(t, 4))
            on(i - 1, lambda t: pass_on(t, 2))
            on(i - 6, lambda t: give(t, 3))

            @pl.when(i + 2 < tiles)
            def _():
                conv_next(i + 2)

            on(i - 2, lambda t: pass_on(t, 3))
            on(i - 7, lambda t: give(t, 2))
            on(i - 10, events_back)
            on(i - 3, lambda t: pass_on(t, 4))
            on(i - 8, lambda t: give(t, 1))
            on(i - 10, tap_sums)
            on(i - 9, settle)
            on(i - 4, meet)
            return 0

        lax.fori_loop(0, tiles + 10, tick, 0)

        sum_all()
        for slot in range(REACH + 1):
            ids_to(slot).wait_send()

        def drain(t, _):
            grads_halo(t).wait_send()
            for d in range(1, REACH + 1):
                fwd(t, d).wait_send()
                back(t, d).wait_send()
            return 0

        def drain_halo(n, _):
            events_halo(n).wait_send()
            return 0

        lax.fori_loop(0, tiles, drain, 0)
        lax.fori_loop(0, tiles // batch, drain_halo, 0)

    vmem = pl.BlockSpec(memory_space=pltpu.VMEM)
    hbm = pl.BlockSpec(memory_space=pl.ANY)
    sems = pltpu.SemaphoreType.DMA
    tall = jax.ShapeDtypeStruct((rows, width), bf16)
    return pl.pallas_call(
        kernel,
        out_shape=(tall, tall, tall, jax.ShapeDtypeStruct((taps, width), f32)),
        in_specs=[hbm] * 4 + [vmem, vmem, hbm],
        out_specs=(vmem,) * 4,
        scratch_shapes=[
            pltpu.VMEM((2, tiles, span, LANES), bf16),
            pltpu.VMEM((2, tiles, span, LANES), f32),
            pltpu.VMEM((2, tiles, span - rows, LANES), bf16),
            pltpu.VMEM((2, tiles, span - rows, LANES), bf16),
            pltpu.VMEM((tiles, RIM, LANES), bf16),
            pltpu.VMEM((tiles, RIM, LANES), bf16),
            pltpu.VMEM((tiles, rows, LANES), bf16),
            pltpu.VMEM((tiles, RIM, LANES), bf16),
            pltpu.VMEM((8, LANES), f32),
            pltpu.VMEM((REACH + 1, 8, LANES), f32),
            pltpu.VMEM((span, 2 * rows), f32),
            pltpu.VMEM((rows, LANES), f32),
            pltpu.VMEM((rows, LANES), f32),
            pltpu.VMEM((rows + RIM, LANES), f32),
            pltpu.VMEM((8, shifted_rows, LANES), f32),
            *[pltpu.VMEM((rows, width), bf16)] * 4,
            pltpu.VMEM((taps, width), f32),
            sems((5,)),
            pltpu.VMEM((taps, LANES), f32),
            pltpu.VMEM((n_dp, piece, LANES), bf16),
            pltpu.VMEM((n_dp, piece, LANES), bf16),
            pltpu.VMEM((piece, LANES), bf16),
            pltpu.VMEM((n_seq, piece, LANES), bf16),
            pltpu.VMEM((piece, LANES), bf16),
            pltpu.VMEM((n_dp, piece, LANES), bf16),
            sems((3,)), sems((3,)),
            sems((tiles, REACH)), sems((tiles, REACH)),
            sems((tiles, REACH)), sems((tiles, REACH)),
            sems((tiles // batch,)), sems((tiles // batch,)), sems((tiles,)), sems((tiles,)),
            sems((REACH + 1,)), sems((REACH + 1,)),
        ],
        compiler_params=pltpu.CompilerParams(
            collective_id=0, has_side_effects=True, vmem_limit_bytes=48 * 1024 * 1024
        ),
        name="timeline",
    )(query, key_rows, feats, grad, ids, picked, weight)


def per_device(queries, keys, events, out_grad, segment_ids, block_list, conv_weight):
    blist = block_list[0]
    here = lax.axis_index("seq")
    own = lax.dynamic_slice_in_dim(blist, here, 1, 0)
    wanted = here - jnp.arange(8, dtype=jnp.int32)
    hit = jnp.any(own == wanted[:, None], axis=1) & (wanted >= 0)
    picked = jnp.broadcast_to(hit.astype(jnp.float32)[:, None], (8, LANES))
    q_grad, k_grad, e_grad, f_grad = timeline(
        queries[0], keys[0], events[0], out_grad[0], segment_ids, picked, conv_weight
    )
    return (q_grad[None], k_grad[None], e_grad[None], f_grad)


def solution(mesh):
    in_specs = (
        P("dp", "seq", None),
        P("dp", "seq", None),
        P("dp", "seq", None),
        P("dp", "seq", None),
        P("dp", "seq"),
        P("dp", None, None),
        P(),
    )
    out_specs = (P("dp", "seq", None), P("dp", "seq", None), P("dp", "seq", None), P())
    return jax.shard_map(
        per_device, mesh=mesh, in_specs=in_specs, out_specs=out_specs, check_vma=False
    )
```

time: 270 us -> 193 us (0.71)
  Pallas kernels: 257 us -> 182 us
    pallas_call x1 -> x0, Pallas kernels: 65 us -> none  [spread_sum(): pl.pallas_call(kernel, out_shape=jax.ShapeDtypeStruct((taps, width), jnp....]
    pallas_call x1, Pallas kernels: 192 us -> 182 us  [timeline(): pl.pallas_call(kernel, out_shape=(tall, tall, tall, jax.ShapeDtypeStruct(...]
    unnamed x22 -> x18, local copies, waits for them, and re-layouts: 10.9 us -> 9.64 us
where the time goes in v3:
time: 193 us
  Pallas kernels  182 us (94%)
  local copies, waits for them, and re-layouts  9.89 us (5%)
    pallas_call x1, Pallas kernels, timeline(): pl.pallas_call(kernel, out_shape=(tall, tall, tall, jax.ShapeDtypeStruct(...  182 us
    unnamed x18, local copies, waits for them, and re-layouts  9.64 us

profile of v3, /device:TPU:1, one launch (start us, length us, event | category | flops | bytes accessed | tf_op | source)
XLA Modules:
  0.0 192.9 jit_solution(3206852843096019549)
XLA Ops:
  0.6 0.0 copy-start
  0.6 0.7 copy-done
  1.3 0.2 dynamic-slice_reduce_fusion
  1.5 0.1 compare_reduce_fusion
  1.6 0.0 copy-start.6
  1.6 0.1 broadcast_in_dim.16.pick_ref
  1.7 0.6 copy-done.6
  2.3 0.0 copy-start.1
  2.3 1.0 copy-done.1
  3.3 0.0 copy-start.2
  3.3 1.0 copy-done.2
  4.3 0.0 copy-start.3
  4.4 1.0 copy-done.3
  5.4 0.0 copy-start.4
  5.4 1.0 copy-done.4
  6.4 0.0 copy-start.5
  6.4 1.0 copy-done.5
  7.5 182.2 %timeline.1 = (bf16[128,2048]{1,0:T(8,128)(2,1)S(1)}, bf16[128,2048]{1,0:T(8,128)(2,1)S(1)}, bf16[128,2048]{1,0:T(8,128)(2,1)S(1)}, f32[64,2048]{1,0:T(8,128)S(1)}) custom-call(bf16[128,2048]{1,0:T(8,128)(2,1)S(1)} %bitcast.10, bf16[128,2048]{1,0:T(8,128)(2,1)S(1)} %bitcast.11, bf16[128,2048]{1,0:T(8,128)(2,1)S(1)} %bitcast.12, ...), custom_call_target="tpu_custom_call" | custom-call | tf_op jit(solution)/shard_map/timeline/pallas_call | solution.py:390
  189.7 0.8 copy.15
  190.5 0.8 copy.16
  191.3 0.8 copy.17
  192.1 0.8 copy.18
  (2 shorter events, 0.0 us)
Async XLA Ops:
  0.6 0.7 copy-start
  1.6 0.7 copy-start.6
  2.3 1.0 copy-start.1
  3.3 1.0 copy-start.2
  4.3 1.0 copy-start.3
  5.4 1.0 copy-start.4
  6.4 1.0 copy-start.5

commit v4 on v3

--- a/solution.py
+++ b/solution.py
@@ -10,6 +10,8 @@
 LANES = 128
 RIM = 64
 BATCH = 4
+PAIR = 2
+QUAD = 4
 MESH = pl.DeviceIdType.MESH
 
 
@@ -19,6 +21,10 @@
     taps = weight.shape[0]
     tiles = width // LANES
     batch = min(BATCH, tiles)
+    half = tiles // PAIR
+    units = 2 * half
+    conv_lag = min(2, half - 1)
+    rounds = n_seq // QUAD
     split = n_dp // tiles
     piece = taps // split
     mean = 1.0 / (n_dp * n_seq)
@@ -33,7 +39,7 @@
         win, part, out_buf, in_buf, e_halo, v_halo, vg, e_src,
         id_src, id_buf, cap, left, right, ext, moved,
         q_ref, k_ref, e_ref, g_ref, w_ref, load_s,
-        f_ref, mine, got, part_sum, got_z, total_sum, whole, sum_s, sum_r,
+        probs_ref, f_ref, mine, got, near, far, near_in, far_in, total_sum, whole, sum_s, sum_r,
         win_s, win_r, back_s, back_r, eh_s, eh_r, vh_s, vh_r, id_s, id_r,
     ):
         me, lane_me = lax.axis_index("seq"), lax.axis_index("dp")
@@ -52,27 +58,30 @@
         def cols(tile):
             return pl.ds(pl.multiple_of(tile * LANES, LANES), LANES)
 
-        def fwd(t, d):
+        def both(u):
+            return pl.ds(u * PAIR, PAIR)
+
+        def fwd(u, d):
             return remote(
-                win.at[:, t, pl.ds((d - 1) * rows, rows), :],
-                win.at[:, t, pl.ds(d * rows, rows), :],
-                win_s.at[t, d - 1], win_r.at[t, d - 1], up,
-            )
-
-        def back(t, d):
+                win.at[both(u), pl.ds((d - 1) * rows, rows), :],
+                win.at[both(u), pl.ds(d * rows, rows), :],
+                win_s.at[u, d - 1], win_r.at[u, d - 1], up,
+            )
+
+        def back(u, d):
             return remote(
-                out_buf.at[:, t, pl.ds((d - 1) * rows, rows), :],
-                in_buf.at[:, t, pl.ds((d - 1) * rows, rows), :],
-                back_s.at[t, d - 1], back_r.at[t, d - 1], down,
+                out_buf.at[both(u), pl.ds((d - 1) * rows, rows), :],
+                in_buf.at[both(u), pl.ds((d - 1) * rows, rows), :],
+                back_s.at[u, d - 1], back_r.at[u, d - 1], down,
             )
 
         def events_halo(n):
             several = pl.ds(n * batch, batch)
             return remote(e_src.at[several], e_halo.at[several], eh_s.at[n], eh_r.at[n], up)
 
-        def grads_halo(t):
+        def grads_halo(u):
             return remote(
-                vg.at[t, pl.ds(0, RIM), :], v_halo.at[t], vh_s.at[t], vh_r.at[t], down
+                vg.at[both(u), pl.ds(0, RIM), :], v_halo.at[both(u)], vh_s.at[u], vh_r.at[u], down
             )
 
         def ids_to(slot):
@@ -107,7 +116,7 @@
             load.wait()
 
         def stage(tile, _):
-            win[0, tile, pl.ds(0, rows), :] = k_ref[:, cols(tile)]
+            win[tile, pl.ds(0, rows), :] = k_ref[:, cols(tile)]
             e_src[tile] = e_ref[pl.ds(rows - RIM, RIM), cols(tile)]
             return 0
 
@@ -116,11 +125,7 @@
         for slot in range(REACH + 1):
             ids_to(slot).start()
 
-        def start_halo(c, _):
-            events_halo(c).start()
-            return 0
-
-        lax.fori_loop(0, tiles // batch, start_halo, 0)
+        fwd(0, 1).start()
         for slot in range(REACH + 1):
             ids_to(slot).wait_recv()
 
@@ -175,7 +180,7 @@
                 return total
 
             total = lax.fori_loop(0, taps // 8, body, jnp.zeros((rows, LANES), f32))
-            win[1, tile, pl.ds(0, rows), :] = total.astype(bf16)
+            win[tiles + tile, pl.ds(0, rows), :] = total.astype(bf16)
 
         def conv_next(tile):
             @pl.when(lax.rem(tile, batch) == 0)
@@ -184,56 +189,68 @@
 
             conv(tile)
 
-        def attend(tile):
-            lane = lax.broadcasted_iota(jnp.int32, (rows, LANES), 1)
-            first = lane < HD
-
-            def pair(ref):
-                both = ref[:, cols(tile)].astype(f32)
-                return jnp.concatenate(
-                    [jnp.where(first, both, 0.0), jnp.where(first, 0.0, both)], axis=0
-                ).astype(bf16)
-
-            q2, g2 = pair(q_ref), pair(g_ref)
-            keys, vals = win[0, tile], win[1, tile]
-            last = (((1,), (1,)), ((), ()))
-            scores = lax.dot_general(keys, q2, last, preferred_element_type=f32)
+        lane = lax.broadcasted_iota(jnp.int32, (rows, LANES), 1)
+        first_head = lane < HD
+        last = (((1,), (1,)), ((), ()))
+        mid = (((1,), (0,)), ((), ()))
+
+        def heads(ref, tile):
+            wide = ref[:, cols(tile)].astype(f32)
+            return jnp.concatenate(
+                [jnp.where(first_head, wide, 0.0), jnp.where(first_head, 0.0, wide)], axis=0
+            ).astype(bf16)
+
+        def attend_keys(tile):
+            scores = lax.dot_general(win[tile], heads(q_ref, tile), last, preferred_element_type=f32)
             scores = jnp.minimum(scores * scale, cap[...])
             top = jnp.max(scores, axis=0, keepdims=True)
             raw = jnp.exp(scores - top)
             probs = raw * (1.0 / jnp.sum(raw, axis=0, keepdims=True))
-            low_probs = probs.astype(bf16)
-            dprobs = lax.dot_general(vals, g2, last, preferred_element_type=f32)
-            delta = jnp.sum(low_probs.astype(f32) * dprobs, axis=0, keepdims=True)
+            probs_ref[tile] = probs
+            part[tile] = lax.dot_general(
+                probs.astype(bf16), heads(g_ref, tile), mid, preferred_element_type=f32
+            )
+
+        def attend_values(tile):
+            keys, vals = win[tile], win[tiles + tile]
+            probs = probs_ref[tile]
+            dprobs = lax.dot_general(vals, heads(g_ref, tile), last, preferred_element_type=f32)
+            low_probs = probs.astype(bf16).astype(f32)
+            delta = jnp.sum(low_probs * dprobs, axis=0, keepdims=True)
             dscores = (probs * (dprobs - delta)).astype(bf16)
+            part[tiles + tile] = scale * lax.dot_general(
+                dscores, heads(q_ref, tile), mid, preferred_element_type=f32
+            )
             dq2 = lax.dot_general(
                 dscores, keys, (((0,), (0,)), ((), ())), preferred_element_type=f32
             )
-            dq = jnp.where(first, dq2[0:rows], dq2[rows : 2 * rows]) * scale
+            dq = jnp.where(first_head, dq2[0:rows], dq2[rows : 2 * rows]) * scale
             dq_ref[:, cols(tile)] = dq.astype(bf16)
-            mid = (((1,), (0,)), ((), ()))
-            part[0, tile] = lax.dot_general(dscores, q2, mid, preferred_element_type=f32) * scale
-            part[1, tile] = lax.dot_general(low_probs, g2, mid, preferred_element_type=f32)
-
-        def give(t, d):
+
+        def give(u, d):
             at_d = pl.ds(d * rows, rows)
-            total = part[:, t, at_d, :]
+            total = part[both(u), at_d, :]
             if d < REACH:
-                back(t, d + 1).wait_recv()
-                total = total + in_buf[:, t, at_d, :].astype(f32)
-            out_buf[:, t, pl.ds((d - 1) * rows, rows), :] = total.astype(bf16)
-            back(t, d).start()
-
-        def settle(t):
-            back(t, 1).wait_recv()
-            total = part[:, t, pl.ds(0, rows), :] + in_buf[:, t, pl.ds(0, rows), :].astype(f32)
-            low_total = total.astype(bf16)
-            dk_ref[:, cols(t)] = low_total[0]
-            vg[t] = low_total[1]
-            grads_halo(t).start()
+                back(u, d + 1).wait_recv()
+                total = total + in_buf[both(u), at_d, :].astype(f32)
+            out_buf[both(u), pl.ds((d - 1) * rows, rows), :] = total.astype(bf16)
+            back(u, d).start()
+
+        def settle(u):
+            back(u, 1).wait_recv()
+            total = part[both(u), pl.ds(0, rows), :] + in_buf[both(u), pl.ds(0, rows), :].astype(f32)
+            return total.astype(bf16)
+
+        def settle_values(u):
+            vg[both(u)] = settle(u)
+            grads_halo(u).start()
+
+        def settle_keys(u):
+            low_total = settle(u)
+            for n in range(PAIR):
+                dk_ref[:, cols((u - half) * PAIR + n)] = low_total[n]
 
         def events_back(tile):
-            grads_halo(tile).wait_recv()
             own = vg[tile].astype(f32)
             ext[0:rows, :] = own
             ext[rows : rows + RIM, :] = v_halo[tile].astype(f32)
@@ -294,97 +311,136 @@
         def settled(ref, n, count):
             pltpu.make_async_copy(ref.at[pl.ds(0, count)], ref.at[pl.ds(0, count)], n).wait()
 
-        def sum_all():
+        my_quad, my_place = lax.div(me, QUAD), lax.rem(me, QUAD)
+
+        def added(ref, count):
+            total = ref[0].astype(f32)
+            for n in range(1, count):
+                total = total + ref[n].astype(f32)
+            return total
+
+        def sum_near():
             settled(got, sum_r.at[0], n_dp - 1)
-            total = got[0].astype(f32)
-            for n in range(1, n_dp):
-                total = total + got[n].astype(f32)
-            part_sum[...] = total.astype(bf16)
-
-            def send_z(n, _):
-                remote(part_sum, got_z.at[me], sum_s.at[1], sum_r.at[1], at(n)).start()
-                return 0
-
-            lax.fori_loop(1, n_seq, send_z, 0)
-            got_z[me] = part_sum[...]
-            settled(got_z, sum_r.at[1], n_seq - 1)
-            total = got_z[0].astype(f32)
-            for n in range(1, n_seq):
-                total = total + got_z[n].astype(f32)
-            total_sum[...] = (total * mean).astype(bf16)
-
-            def send_dp(n, _):
-                to_dp(total_sum, whole.at[lane_me], 2, lax.rem(lane_me + n, n_dp)).start()
-                return 0
-
-            lax.fori_loop(1, n_dp, send_dp, 0)
+            near[...] = added(got, n_dp).astype(bf16)
+            near_in[my_place] = near[...]
+            for n in range(1, QUAD):
+                to = my_quad * QUAD + lax.rem(my_place + n, QUAD)
+                remote(near, near_in.at[my_place], sum_s.at[1], sum_r.at[1], to).start()
+
+        def sum_far():
+            settled(near_in, sum_r.at[1], QUAD - 1)
+            far[...] = added(near_in, QUAD).astype(bf16)
+            far_in[my_quad] = far[...]
+            for n in range(1, rounds):
+                remote(far, far_in.at[my_quad], sum_s.at[2], sum_r.at[2], at(n * QUAD)).start()
+
+        def send_dp(n, _):
+            to_dp(total_sum, whole.at[lane_me], 3, lax.rem(lane_me + n, n_dp)).start()
+            return 0
+
+        def sum_out():
+            settled(far_in, sum_r.at[2], rounds - 1)
+            total_sum[...] = (added(far_in, rounds) * mean).astype(bf16)
             whole[lane_me] = total_sum[...]
-            settled(whole, sum_r.at[2], n_dp - 1)
+            lax.fori_loop(1, n_dp // 2, send_dp, 0)
+
+        def sum_end():
+            settled(whole, sum_r.at[3], n_dp - 1)
             for n in range(n_dp):
                 col, row = (n // split) * LANES, (n % split) * piece
                 f_out[row : row + piece, col : col + LANES] = whole[n].astype(f32)
             settled(mine, sum_s.at[0], n_dp - 1)
-            settled(got_z, sum_s.at[1], n_seq - 1)
-            settled(whole, sum_s.at[2], n_dp - 1)
-
-        conv_next(0)
-        conv_next(1)
+            settled(near_in, sum_s.at[1], QUAD - 1)
+            settled(far_in, sum_s.at[2], rounds - 1)
+            settled(whole, sum_s.at[3], n_dp - 1)
+
+        def each(act, first):
+            def body(n, _):
+                act(first + n)
+                return 0
+
+            lax.fori_loop(0, PAIR, body, 0)
+
+        def meet_keys(u):
+            fwd(u, REACH).wait_recv()
+            for n in range(PAIR):
+                attend_keys(u * PAIR + n)
+
+        def meet_values(u):
+            fwd(u, REACH).wait_recv()
+            for n in range(PAIR):
+                attend_values((u - half) * PAIR + n)
+
+        def values_done(u):
+            settle_values(u)
+            each(tap_sums, u * PAIR)
+
+        def events_pair(u):
+            grads_halo(u).wait_recv()
+            each(events_back, u * PAIR)
+
+        def pass_on(u, d):
+            fwd(u, d - 1).wait_recv()
+            fwd(u, d).start()
+
+        summed = half + 8
 
         def tick(i, _):
-            def on(t, act):
-                @pl.when(jnp.logical_and(t >= 0, t < tiles))
+            def on(u, act, low_end=0, high_end=units):
+                @pl.when(jnp.logical_and(u >= low_end, u < high_end))
                 def _():
-                    act(t)
-
-            def pass_on(t, d):
-                fwd(t, d - 1).wait_recv()
-                fwd(t, d).start()
-
-            def meet(t):
-                fwd(t, REACH).wait_recv()
-                attend(t)
-
-            on(i, lambda t: fwd(t, 1).start())
-            on(i - 5, lambda t: give(t, 4))
-            on(i - 1, lambda t: pass_on(t, 2))
-            on(i - 6, lambda t: give(t, 3))
-
-            @pl.when(i + 2 < tiles)
+                    act(u)
+
+            on(i, lambda u: fwd(u, 1).start(), low_end=1)
+            on(i, lambda n: events_halo(n).start(), high_end=tiles // batch)
+            on(i - 5, lambda u: give(u, 4))
+            on(i - 1, lambda u: pass_on(u, 2))
+            on(i - 6, lambda u: give(u, 3))
+            on(i - conv_lag, lambda p: each(conv_next, p * PAIR), high_end=half)
+            on(i - 2, lambda u: pass_on(u, 3))
+            on(i - 7, lambda u: give(u, 2))
+            on(i - 10, events_pair, high_end=half)
+            on(i - 3, lambda u: pass_on(u, 4))
+            on(i - 8, lambda u: give(u, 1))
+            on(i - 9, values_done, high_end=half)
+            on(i - 9, settle_keys, low_end=half)
+            pl.when(i == summed + 2)(sum_near)
+            pl.when(i == summed + 3)(sum_far)
+            pl.when(i == summed + 5)(sum_out)
+
+            @pl.when(i == summed + 6)
             def _():
-                conv_next(i + 2)
-
-            on(i - 2, lambda t: pass_on(t, 3))
-            on(i - 7, lambda t: give(t, 2))
-            on(i - 10, events_back)
-            on(i - 3, lambda t: pass_on(t, 4))
-            on(i - 8, lambda t: give(t, 1))
-            on(i - 10, tap_sums)
-            on(i - 9, settle)
-            on(i - 4, meet)
-            return 0
-
-        lax.fori_loop(0, tiles + 10, tick, 0)
-
-        sum_all()
+                lax.fori_loop(n_dp // 2, n_dp, send_dp, 0)
+
+            on(i - 4, meet_keys, high_end=half)
+            on(i - 4, meet_values, low_end=half)
+            return 0
+
+        lax.fori_loop(0, max(units + 9, summed + 7), tick, 0)
+        sum_end()
         for slot in range(REACH + 1):
             ids_to(slot).wait_send()
 
-        def drain(t, _):
-            grads_halo(t).wait_send()
+        def drain(u, _):
             for d in range(1, REACH + 1):
-                fwd(t, d).wait_send()
-                back(t, d).wait_send()
+                fwd(u, d).wait_send()
+                back(u, d).wait_send()
+            return 0
+
+        def drain_grads(u, _):
+            grads_halo(u).wait_send()
             return 0
 
         def drain_halo(n, _):
             events_halo(n).wait_send()
             return 0
 
-        lax.fori_loop(0, tiles, drain, 0)
+        lax.fori_loop(0, units, drain, 0)
+        lax.fori_loop(0, half, drain_grads, 0)
         lax.fori_loop(0, tiles // batch, drain_halo, 0)
 
     vmem = pl.BlockSpec(memory_space=pltpu.VMEM)
-    hbm = pl.BlockSpec(memory_space=pl.ANY)
+    hbm = pl.BlockSpec(memory_space=pltpu.HBM)
     sems = pltpu.SemaphoreType.DMA
     tall = jax.ShapeDtypeStruct((rows, width), bf16)
     return pl.pallas_call(
@@ -393,10 +449,10 @@
         in_specs=[hbm] * 4 + [vmem, vmem, hbm],
         out_specs=(vmem,) * 4,
         scratch_shapes=[
-            pltpu.VMEM((2, tiles, span, LANES), bf16),
-            pltpu.VMEM((2, tiles, span, LANES), f32),
-            pltpu.VMEM((2, tiles, span - rows, LANES), bf16),
-            pltpu.VMEM((2, tiles, span - rows, LANES), bf16),
+            pltpu.VMEM((2 * tiles, span, LANES), bf16),
+            pltpu.VMEM((2 * tiles, span, LANES), f32),
+            pltpu.VMEM((2 * tiles, span - rows, LANES), bf16),
+            pltpu.VMEM((2 * tiles, span - rows, LANES), bf16),
             pltpu.VMEM((tiles, RIM, LANES), bf16),
             pltpu.VMEM((tiles, RIM, LANES), bf16),
             pltpu.VMEM((tiles, rows, LANES), bf16),
@@ -411,17 +467,20 @@
             *[pltpu.VMEM((rows, width), bf16)] * 4,
             pltpu.VMEM((taps, width), f32),
             sems((5,)),
+            pltpu.VMEM((tiles, span, 2 * rows), f32),
             pltpu.VMEM((taps, LANES), f32),
             pltpu.VMEM((n_dp, piece, LANES), bf16),
             pltpu.VMEM((n_dp, piece, LANES), bf16),
             pltpu.VMEM((piece, LANES), bf16),
-            pltpu.VMEM((n_seq, piece, LANES), bf16),
+            pltpu.VMEM((piece, LANES), bf16),
+            pltpu.VMEM((QUAD, piece, LANES), bf16),
+            pltpu.VMEM((rounds, piece, LANES), bf16),
             pltpu.VMEM((piece, LANES), bf16),
             pltpu.VMEM((n_dp, piece, LANES), bf16),
-            sems((3,)), sems((3,)),
-            sems((tiles, REACH)), sems((tiles, REACH)),
-            sems((tiles, REACH)), sems((tiles, REACH)),
-            sems((tiles // batch,)), sems((tiles // batch,)), sems((tiles,)), sems((tiles,)),
+            sems((4,)), sems((4,)),
+            sems((units, REACH)), sems((units, REACH)),
+            sems((units, REACH)), sems((units, REACH)),
+            sems((tiles // batch,)), sems((tiles // batch,)), sems((half,)), sems((half,)),
             sems((REACH + 1,)), sems((REACH + 1,)),
         ],
         compiler_params=pltpu.CompilerParams(

time: 193 us -> 167 us (0.87)
  Pallas kernels: 182 us -> 156 us
    pallas_call x1, Pallas kernels: 182 us -> 156 us  [timeline(): pl.pallas_call(kernel, out_shape=(tall, tall, tall, jax.ShapeDtypeStruct(...]
where the time goes in v4:
time: 167 us
  Pallas kernels  156 us (93%)
  local copies, waits for them, and re-layouts  9.89 us (6%)
    pallas_call x1, Pallas kernels, timeline(): pl.pallas_call(kernel, out_shape=(tall, tall, tall, jax.ShapeDtypeStruct(...  156 us
    unnamed x18, local copies, waits for them, and re-layouts  9.64 us

profile of v4, /device:TPU:1, one launch (start us, length us, event | category | flops | bytes accessed | tf_op | source)
XLA Modules:
  0.0 166.8 jit_solution(11346769466208095287)
XLA Ops:
  0.6 0.0 copy-start
  0.6 0.7 copy-done
  1.3 0.2 dynamic-slice_reduce_fusion
  1.5 0.1 compare_reduce_fusion
  1.6 0.0 copy-start.6
  1.6 0.1 broadcast_in_dim.16.pick_ref
  1.7 0.6 copy-done.6
  2.3 0.0 copy-start.1
  2.3 1.0 copy-done.1
  3.3 0.0 copy-start.2
  3.3 1.0 copy-done.2
  4.3 0.0 copy-start.3
  4.4 1.0 copy-done.3
  5.4 0.0 copy-start.4
  5.4 1.0 copy-done.4
  6.4 0.0 copy-start.5
  6.4 1.0 copy-done.5
  7.5 156.1 %timeline.1 = (bf16[128,2048]{1,0:T(8,128)(2,1)S(1)}, bf16[128,2048]{1,0:T(8,128)(2,1)S(1)}, bf16[128,2048]{1,0:T(8,128)(2,1)S(1)}, f32[64,2048]{1,0:T(8,128)S(1)}) custom-call(bf16[128,2048]{1,0:T(8,128)(2,1)S(1)} %bitcast.10, bf16[128,2048]{1,0:T(8,128)(2,1)S(1)} %bitcast.11, bf16[128,2048]{1,0:T(8,128)(2,1)S(1)} %bitcast.12, ...), custom_call_target="tpu_custom_call" | custom-call | tf_op jit(solution)/shard_map/timeline/pallas_call | solution.py:446
  163.6 0.8 copy.15
  164.4 0.8 copy.16
  165.2 0.8 copy.17
  166.0 0.8 copy.18
  (2 shorter events, 0.0 us)
Async XLA Ops:
  0.6 0.7 copy-start
  1.6 0.7 copy-start.6
  2.3 1.0 copy-start.1
  3.3 1.0 copy-start.2
  4.3 1.0 copy-start.3
  5.4 1.0 copy-start.4
  6.4 1.0 copy-start.5

commit v5 on v4

--- a/solution.py
+++ b/solution.py
@@ -15,7 +15,7 @@
 MESH = pl.DeviceIdType.MESH
 
 
-def timeline(query, key_rows, feats, grad, ids, picked, weight):
+def timeline(query, key_rows, feats, grad, ids, blist, weight):
     n_dp, n_seq = lax.axis_size("dp"), lax.axis_size("seq")
     rows, width = query.shape
     taps = weight.shape[0]
@@ -34,7 +34,7 @@
     f32, bf16 = jnp.float32, jnp.bfloat16
 
     def kernel(
-        q_in, k_in, e_in, g_in, id_ref, pick_ref, w_in,
+        q_in, k_in, e_in, g_in, id_ref, list_ref, w_in,
         dq_ref, dk_ref, de_ref, f_out,
         win, part, out_buf, in_buf, e_halo, v_halo, vg, e_src,
         id_src, id_buf, cap, left, right, ext, moved,
@@ -147,9 +147,13 @@
         reach_right = jnp.sum(high, axis=0, keepdims=True) + jnp.sum(after, axis=0, keepdims=True) - 1.0
         left[...] = jnp.broadcast_to(reach_left, square).T
         right[...] = jnp.broadcast_to(reach_right, square).T
+        listed = list_ref[pl.ds(me, 1), :]
         for d in range(REACH + 1):
             open_pairs = low if d == 0 else same(id_buf[d][0:1])
-            open_pairs = open_pairs * jnp.broadcast_to(pick_ref[d : d + 1, :], square)
+            wanted = jnp.where(listed == me - d, 1.0, 0.0)
+            open_pairs = open_pairs * jnp.broadcast_to(
+                jnp.max(wanted, axis=1, keepdims=True), square
+            )
             limit = jnp.where(open_pairs > 0.5, 3.0e38, -1.0e30)
             cap[d * rows : (d + 1) * rows, 0:rows] = limit
             cap[d * rows : (d + 1) * rows, rows : 2 * rows] = limit
@@ -393,17 +397,17 @@
 
             on(i, lambda u: fwd(u, 1).start(), low_end=1)
             on(i, lambda n: events_halo(n).start(), high_end=tiles // batch)
+            on(i - 1, lambda u: pass_on(u, 2))
             on(i - 5, lambda u: give(u, 4))
-            on(i - 1, lambda u: pass_on(u, 2))
+            on(i - 2, lambda u: pass_on(u, 3))
             on(i - 6, lambda u: give(u, 3))
+            on(i - 3, lambda u: pass_on(u, 4))
+            on(i - 7, lambda u: give(u, 2))
+            on(i - 8, lambda u: give(u, 1))
             on(i - conv_lag, lambda p: each(conv_next, p * PAIR), high_end=half)
-            on(i - 2, lambda u: pass_on(u, 3))
-            on(i - 7, lambda u: give(u, 2))
-            on(i - 10, events_pair, high_end=half)
-            on(i - 3, lambda u: pass_on(u, 4))
-            on(i - 8, lambda u: give(u, 1))
             on(i - 9, values_done, high_end=half)
             on(i - 9, settle_keys, low_end=half)
+            on(i - 11, events_pair, high_end=half)
             pl.when(i == summed + 2)(sum_near)
             pl.when(i == summed + 3)(sum_far)
             pl.when(i == summed + 5)(sum_out)
@@ -484,21 +488,15 @@
             sems((REACH + 1,)), sems((REACH + 1,)),
         ],
         compiler_params=pltpu.CompilerParams(
-            collective_id=0, has_side_effects=True, vmem_limit_bytes=48 * 1024 * 1024
+            collective_id=0, has_side_effects=True, vmem_limit_bytes=63 * 1024 * 1024
         ),
         name="timeline",
-    )(query, key_rows, feats, grad, ids, picked, weight)
+    )(query, key_rows, feats, grad, ids, blist, weight)
 
 
 def per_device(queries, keys, events, out_grad, segment_ids, block_list, conv_weight):
-    blist = block_list[0]
-    here = lax.axis_index("seq")
-    own = lax.dynamic_slice_in_dim(blist, here, 1, 0)
-    wanted = here - jnp.arange(8, dtype=jnp.int32)
-    hit = jnp.any(own == wanted[:, None], axis=1) & (wanted >= 0)
-    picked = jnp.broadcast_to(hit.astype(jnp.float32)[:, None], (8, LANES))
     q_grad, k_grad, e_grad, f_grad = timeline(
-        queries[0], keys[0], events[0], out_grad[0], segment_ids, picked, conv_weight
+        queries[0], keys[0], events[0], out_grad[0], segment_ids, block_list[0], conv_weight
     )
     return (q_grad[None], k_grad[None], e_grad[None], f_grad)
 

time: 167 us -> 165 us (0.988)
  local copies, waits for them, and re-layouts: 9.89 us -> 6.55 us
    unnamed x18 -> x12, local copies, waits for them, and re-layouts: 9.64 us -> 5.87 us
where the time goes in v5:
time: 165 us
  Pallas kernels  157 us (95%)
  local copies, waits for them, and re-layouts  6.55 us (4%)
    pallas_call x1, Pallas kernels, timeline(): pl.pallas_call(kernel, out_shape=(tall, tall, tall, jax.ShapeDtypeStruct(...  157 us
    unnamed x12, local copies, waits for them, and re-layouts  5.87 us

profile of v5, /device:TPU:1, one launch (start us, length us, event | category | flops | bytes accessed | tf_op | source)
XLA Modules:
  0.0 164.6 jit_solution(4315573261140498012)
XLA Ops:
  0.6 0.0 copy-start.3
  0.6 0.7 copy-done.3
  1.3 0.7 copy.11.list_ref
  2.0 157.4 %timeline.1 = (bf16[128,2048]{1,0:T(8,128)(2,1)}, bf16[128,2048]{1,0:T(8,128)(2,1)}, bf16[128,2048]{1,0:T(8,128)(2,1)}, f32[64,2048]{1,0:T(8,128)}) custom-call(bf16[128,2048]{1,0:T(8,128)(2,1)} %bitcast.11, bf16[128,2048]{1,0:T(8,128)(2,1)} %bitcast.12, bf16[128,2048]{1,0:T(8,128)(2,1)} %bitcast.13, bf16[128,2048]{1,0:T(8,128)(2,1)} %bitcast.14, ...), custom_call_target="tpu_custom_call" | custom-call | tf_op jit(solution)/shard_map/timeline/pallas_call | solution.py:450
  159.4 0.0 copy-start.2
  159.5 1.9 %copy.16 = bf16[1,128,2048]{2,1,0:T(8,128)(2,1)} copy(bf16[1,128,2048]{2,1,0:T(8,128)(2,1)} %bitcast.10) | data formatting | bytes 1048576
  161.4 0.0 copy-done.2
  161.4 0.0 copy-start.1
  161.4 0.8 copy.17
  162.2 0.4 copy-done.1
  162.6 0.0 copy-start
  162.6 0.8 copy.18
  163.4 0.4 copy-done
  163.9 0.8 copy.19
Async XLA Ops:
  0.6 0.7 copy-start.3
  159.4 2.0 %copy-start.2 = (bf16[128,2048]{1,0:T(8,128)(2,1)S(1)}, bf16[128,2048]{1,0:T(8,128)(2,1)}, u32[]{:S(2)}) copy-start(bf16[128,2048]{1,0:T(8,128)(2,1)} %get-tuple-element.9) | copy-start | bytes 1572868
  161.4 1.2 copy-start.1
  162.6 1.2 copy-start

commit v6 on v5

--- a/solution.py
+++ b/solution.py
@@ -147,10 +147,12 @@
         reach_right = jnp.sum(high, axis=0, keepdims=True) + jnp.sum(after, axis=0, keepdims=True) - 1.0
         left[...] = jnp.broadcast_to(reach_left, square).T
         right[...] = jnp.broadcast_to(reach_right, square).T
-        listed = list_ref[pl.ds(me, 1), :]
+        listed = list_ref[...]
+        mine_at = lax.broadcasted_iota(jnp.int32, listed.shape, 1) == me
         for d in range(REACH + 1):
             open_pairs = low if d == 0 else same(id_buf[d][0:1])
-            wanted = jnp.where(listed == me - d, 1.0, 0.0)
+            wanted = jnp.where(mine_at & (listed == me - d), 1.0, 0.0)
+            wanted = jnp.max(wanted, axis=0, keepdims=True)
             open_pairs = open_pairs * jnp.broadcast_to(
                 jnp.max(wanted, axis=1, keepdims=True), square
             )
@@ -488,7 +490,7 @@
             sems((REACH + 1,)), sems((REACH + 1,)),
         ],
         compiler_params=pltpu.CompilerParams(
-            collective_id=0, has_side_effects=True, vmem_limit_bytes=63 * 1024 * 1024
+            collective_id=0, has_side_effects=True, vmem_limit_bytes=52 * 1024 * 1024
         ),
         name="timeline",
     )(query, key_rows, feats, grad, ids, blist, weight)
@@ -496,7 +498,7 @@
 
 def per_device(queries, keys, events, out_grad, segment_ids, block_list, conv_weight):
     q_grad, k_grad, e_grad, f_grad = timeline(
-        queries[0], keys[0], events[0], out_grad[0], segment_ids, block_list[0], conv_weight
+        queries[0], keys[0], events[0], out_grad[0], segment_ids, block_list[0].T, conv_weight
     )
     return (q_grad[None], k_grad[None], e_grad[None], f_grad)
 

time: 165 us -> 162 us (0.982)
  local copies, waits for them, and re-layouts: 6.55 us -> 4.28 us
    unnamed x12 -> x10, local copies, waits for them, and re-layouts: 5.87 us -> 4.28 us
where the time goes in v6:
time: 162 us; the launch traced here: 161 us
  Pallas kernels  156 us (96%)
  local copies, waits for them, and re-layouts  4.28 us (3%)
    pallas_call x1, Pallas kernels, timeline(): pl.pallas_call(kernel, out_shape=(tall, tall, tall, jax.ShapeDtypeStruct(...  156 us
    unnamed x10, local copies, waits for them, and re-layouts  4.28 us

profile of v6, /device:TPU:1, one launch (start us, length us, event | category | flops | bytes accessed | tf_op | source)
XLA Modules:
  0.0 161.3 jit_solution(7806436511751288316)
XLA Ops:
  0.6 0.0 copy-start
  0.6 0.0 copy-start.1
  0.7 0.7 copy-done
  1.3 0.0 copy-done.1
  1.3 156.4 %timeline.1 = (bf16[128,2048]{1,0:T(8,128)(2,1)S(1)}, bf16[128,2048]{1,0:T(8,128)(2,1)S(1)}, bf16[128,2048]{1,0:T(8,128)(2,1)S(1)}, f32[64,2048]{1,0:T(8,128)}) custom-call(bf16[128,2048]{1,0:T(8,128)(2,1)} %bitcast.14, bf16[128,2048]{1,0:T(8,128)(2,1)} %bitcast.15, bf16[128,2048]{1,0:T(8,128)(2,1)} %bitcast.16, bf16[128,2048]{1,0:T(8,128)(2,1)} %bitcast.17, ...), custom_call_target="tpu_custom_call" | custom-call | tf_op jit(solution)/shard_map/timeline/pallas_call | solution.py:452
  157.7 0.8 copy.15
  158.5 0.8 copy.16
  159.3 0.0 copy-start.2
  159.3 0.8 copy.17
  160.1 0.4 copy-done.2
  160.5 0.8 copy.18
Async XLA Ops:
  0.6 0.7 copy-start
  0.6 0.7 copy-start.1
  159.3 1.2 copy-start.2
